TPU v7x, 256 devices: a whole 4x4x8 slice. The times are simulated.
256 devices in a mesh: req: 32 (over x, y, core), kv: 8 (over z).
Axes of the slice: x: 4, y: 4, z: 8, core: 2. Of those that a mesh axis runs over, the one named last changes fastest.
Arguments:
- queries: bfloat16 [256, 4096], P(('req', 'kv')), may hold values from -16 to 16
- paged_key_cache: bfloat16 [1536, 128, 1024], P(('req', 'kv')), may hold values from -8 to 8
- paged_value_cache: bfloat16 [1536, 128, 1024], P(('req', 'kv')), may hold values from -6 to 6
- page_request: int32 [1536], P(('req', 'kv')), may hold values from 0 to 255, as said below
- page_number: int32 [1536], P(('req', 'kv')), may hold values from 0 to 23, as said below
- lengths: int32 [256], replicated, may hold values from 1 to 3072, as said below
Outputs:
- attended: bfloat16 [256, 4096], P(('req', 'kv'))
Inputs may be any that keep to these rules, and one draw needn't show every extreme that they name: `page_request`: every request has 1 to 24 pages and some request exactly 24; the 6 slots of one device hold pages of requests r with 6 different values of r // 8. `page_number`: the pages of one request are numbered 0, 1, 2 and so on without gaps, each number once. `lengths`: a request with n pages has a length from (n - 1) * 128 + 1 to n * 128.
All inputs are finite; a program needn't handle non-finite values.
Results may differ from a plain program's by a relative error of at most 0.0023.
Values may be sent and summed in bfloat16 or wider, within the bound.
No kernel may reach another device: no remote copies, remote signals or barrier semaphores. Data moves between devices by JAX's collectives and lax.ppermute only.
A program may use at most 64 MiB of HBM per device.

v0:
```python
import math

import jax
import jax.numpy as jnp
from jax import lax
from jax.sharding import PartitionSpec as P

HQ = 32
KEY_VALUE_HEADS = 8
HEAD_SIZE = 128
QUERY_PER_KV = 4


lowest = -1e30


def sent_to_all(array, axis):
    copies = jnp.broadcast_to(array, (lax.axis_size(axis), *array.shape))
    return lax.all_to_all(copies, axis, split_axis=0, concat_axis=0, tiled=True)


def joined_along(tiles, dim):
    dims = list(tiles.shape[1:])
    dims[dim] *= tiles.shape[0]
    return jnp.moveaxis(tiles, 0, dim).reshape(dims)


def gather_directly(array, axis, dim):
    tiles = sent_to_all(array, axis)
    return joined_along(tiles, dim)


def in_one_piece(arrays, axis, split_dim, concat_dim, along):
    widths = [math.prod(a.shape[along:]) for a in arrays]
    both = jnp.concatenate(
        [a.reshape(*a.shape[:along], w) for a, w in zip(arrays, widths)], axis=along
    )
    out = lax.all_to_all(both, axis, split_axis=split_dim, concat_axis=concat_dim, tiled=True)
    tiles = jnp.split(out, [sum(widths[:k]) for k in range(1, len(widths))], axis=along)
    return tuple((b.reshape(*out.shape[:along], *a.shape[along:]) for a, b in zip(arrays, tiles)))


def in_one_piece_2(arrays, axis, split_dim, concat_dim, along):
    both = jnp.concatenate(arrays, axis=along)
    out, at, gathered = (
        lax.all_to_all(both, axis, split_axis=split_dim, concat_axis=concat_dim, tiled=True),
        0,
        [],
    )
    for a in arrays:
        gathered.append(lax.slice_in_dim(out, at, at + a.shape[along], axis=along))
        at += a.shape[along]
    return tuple(gathered)


def page_attention(gathered_query_rows, gathered_key_rows, gathered_value_rows, usable):
    token_count, page_token_count, _ = gathered_key_rows.shape
    query_half = gathered_query_rows.reshape(token_count, KEY_VALUE_HEADS, QUERY_PER_KV, HEAD_SIZE)
    key_half = gathered_key_rows.reshape(token_count, page_token_count, KEY_VALUE_HEADS, HEAD_SIZE)
    value_half = gathered_value_rows.reshape(
        token_count, page_token_count, KEY_VALUE_HEADS, HEAD_SIZE
    )
    scores = jnp.einsum(
        "sgqd,stgd->sgqt", query_half, key_half, preferred_element_type=jnp.float32
    ) * HEAD_SIZE ** (-0.5)
    scores = jnp.where(usable[:, None, None, :], scores, lowest)
    maxima = jnp.max(scores, axis=-1)
    weights = jnp.exp(scores - maxima[..., None])
    sums_exp = jnp.sum(weights, axis=-1)
    rounded = weights.astype(jnp.bfloat16)
    partial_out = jnp.einsum(
        "sgqt,stgd->sgqd", rounded, value_half, preferred_element_type=jnp.float32
    )
    return (
        maxima.reshape(token_count, HQ),
        sums_exp.reshape(token_count, HQ),
        partial_out.reshape(token_count, HQ * HEAD_SIZE),
    )


def collect(member, factors, partial_out, sums_exp):
    token_count = partial_out.shape[0]
    scaled = (factors[:, :, None] * partial_out.reshape(token_count, HQ, HEAD_SIZE)).reshape(
        token_count, HQ * HEAD_SIZE
    )
    numerators = jnp.einsum("sr,sc->rc", member, scaled, precision=lax.Precision.HIGHEST)
    denominators = jnp.einsum(
        "sr,sc->rc", member, factors * sums_exp, precision=lax.Precision.HIGHEST
    )
    return (numerators, denominators)


def combine_rows(matches, maxima, outputs, sums_exp):
    member = matches.astype(jnp.float32)
    merged_max = jnp.max(jnp.where(matches[:, :, None], maxima[:, None, :], lowest), axis=0)
    row_max = jnp.max(jnp.where(matches[:, :, None], merged_max[None, :, :], lowest), axis=1)
    factors = jnp.exp(maxima - row_max)
    numerators, denominators = collect(member, factors, outputs, sums_exp)
    return (merged_max, numerators, denominators)


def on_device(queries, paged_key_cache, paged_value_cache, page_request, page_number, lengths):
    own_rows = queries.shape[0]
    page_token_count = paged_key_cache.shape[1]
    requests_all = lengths.shape[0]
    groups_req = lax.axis_size("req")
    groups_kv = lax.axis_size("kv")
    group_size = requests_all // groups_req
    group_query = gather_directly(queries, "kv", 0)
    owner_group = page_request // group_size
    within_group = page_request % group_size
    group_hits = owner_group[:, None] == jnp.arange(groups_req, dtype=jnp.int32)[None, :]
    wanted = jnp.sum(jnp.where(group_hits, within_group[:, None], 0), axis=0)
    asked = lax.all_to_all(
        wanted.reshape(groups_req, 1), "req", split_axis=0, concat_axis=0, tiled=True
    )
    picked = jnp.take(group_query, asked[:, 0], axis=0)
    answered = lax.all_to_all(picked, "req", split_axis=0, concat_axis=0, tiled=True)
    gathered_query_rows = jnp.take(answered, owner_group, axis=0)
    limits = jnp.take(lengths, page_request)
    positions = jnp.arange(page_token_count, dtype=jnp.int32)
    usable = page_number[:, None] * page_token_count + positions[None, :] < limits[:, None]
    maxima, sums_exp, partial_out = page_attention(
        gathered_query_rows, paged_key_cache, paged_value_cache, usable
    )
    target = page_request // group_size
    inside = (page_request % group_size).astype(jnp.float32)
    places = target[:, None] == jnp.arange(groups_req, dtype=jnp.int32)[None, :]
    place_f = places.astype(jnp.float32)
    out_sent = jnp.einsum("sg,sc->gc", place_f, partial_out, precision=lax.Precision.HIGHEST)
    sum_sent = jnp.einsum("sg,sc->gc", place_f, sums_exp, precision=lax.Precision.HIGHEST)
    index_sent = jnp.einsum("sg,s->g", place_f, inside, precision=lax.Precision.HIGHEST)
    max_sent = jnp.max(jnp.where(places[:, :, None], maxima[:, None, :], lowest), axis=0)
    out_in, max_in, sum_in, index_in = in_one_piece(
        (out_sent, max_sent, sum_sent, index_sent), "req", 0, 0, 1
    )
    within = index_in[:, None] == jnp.arange(group_size, dtype=jnp.float32)[None, :]
    group_max, group_numer, group_denom = combine_rows(within, max_in, out_in, sum_in)
    numer_split = group_numer.reshape(groups_kv, own_rows, HQ * HEAD_SIZE)
    denom_split = group_denom.reshape(groups_kv, own_rows, HQ)
    max_split = group_max.reshape(groups_kv, own_rows, HQ)
    numer_in, denom_in, max_back = in_one_piece_2(
        (numer_split, denom_split, max_split), "kv", 0, 0, 2
    )
    request_max = jnp.max(max_back, axis=0)
    rescale = jnp.exp(max_back - request_max[None])
    numer_heads = numer_in.reshape(groups_kv, own_rows, HQ, HEAD_SIZE)
    numerators = jnp.sum(rescale[..., None] * numer_heads, axis=0).reshape(own_rows, HQ * HEAD_SIZE)
    denominators = jnp.sum(rescale * denom_in, axis=0)
    attended = numerators.reshape(own_rows, HQ, HEAD_SIZE) / denominators[:, :, None]
    return attended.reshape(own_rows, HQ * HEAD_SIZE).astype(jnp.bfloat16)


def solution(mesh):
    placed = (
        P(("req", "kv"), None),
        P(("req", "kv"), None, None),
        P(("req", "kv"), None, None),
        P(("req", "kv")),
        P(("req", "kv")),
        P(),
    )
    return jax.shard_map(
        on_device, mesh=mesh, in_specs=placed, out_specs=P(("req", "kv"), None), check_vma=False
    )
```

profile of v0, /device:TPU:1, one launch (start us, length us, event | category | flops | bytes accessed | tf_op | source)
XLA Modules:
  0.0 87.7 jit_solution(10403977942151424023)
XLA Ops:
  0.0 0.8 compare_select_fusion.3
  0.8 0.7 compare_and_fusion.1
  1.5 1.3 %gather_fusion = s32[6]{0:T(128)S(1)} fusion(s32[256]{0:T(256)} %param.11, s32[1024]{0:T(1024)S(1)} %pad_clamp_fusion.2), kind=kCustom, calls=%fused_computation | custom fusion | bytes 72 | tf_op jit(solution)/shard_map/jit(_take)/gather | solution.py:120
  2.8 0.7 and_select_fusion.1
  3.6 0.7 copy.29
  4.3 8.6 %all-to-all-start = ((s32[32,1,1]{2,1,0:T(1,128)}), s32[32,1,1]{2,1,0:T(1,128)S(1)}, u32[]{:S(2)}, u32[]{:S(2)}) async-start(s32[32,1,1]{2,1,0:T(1,128)} %copy.29), calls=%async_computation | async-start | bytes 32768 | tf_op jit(solution)/shard_map/all_to_all | solution.py:114
  13.0 0.8 reduce.5
  13.9 0.5 broadcast.207
  14.4 1.0 %reduce.9 = bf16[8,4096]{1,0:T(8,128)(2,1)S(1)} reduce(bf16[8,1,4096]{2,1,0:T(2,128)(2,1)S(1)} %broadcast_in_dim.137, bf16[]{:T(256)} %broadcast.207), dimensions={1}, to_apply=%broadcast_in_dim.137.reduce_sub_computation | reduce | bytes 131074 | tf_op jit(solution)/shard_map/broadcast_in_dim | solution.py:18
  15.4 0.7 reshape.287
  16.0 3.7 %all-to-all-done = s32[32,1,1]{2,1,0:T(1,128)S(1)} async-done(((s32[32,1,1]{2,1,0:T(1,128)}), s32[32,1,1]{2,1,0:T(1,128)S(1)}, u32[]{:S(2)}, u32[]{:S(2)}) %all-to-all-start) | async-done | bytes 160 | tf_op jit(solution)/shard_map/all_to_all | solution.py:114
  19.7 8.2 %all-to-all-start.1 = ((bf16[8,2,2048]{2,1,0:T(2,128)(2,1)}), bf16[8,2,2048]{2,1,0:T(2,128)(2,1)S(1)}, u32[]{:S(2)}, u32[]{:S(2)}) async-start(bf16[8,2,2048]{2,1,0:T(2,128)(2,1)} %reshape.287), calls=%async_computation.1 | async-start | bytes 131072 | tf_op jit(solution)/shard_map/all_to_all | solution.py:19
  27.9 0.7 reduce.4
  28.6 6.6 %all-to-all-done.1 = bf16[8,2,2048]{2,1,0:T(2,128)(2,1)S(1)} async-done(((bf16[8,2,2048]{2,1,0:T(2,128)(2,1)}), bf16[8,2,2048]{2,1,0:T(2,128)(2,1)S(1)}, u32[]{:S(2)}, u32[]{:S(2)}) %all-to-all-start.1) | async-done | bytes 65568 | tf_op jit(solution)/shard_map/all_to_all | solution.py:19
  35.4 0.7 gather_fusion.1
  36.2 0.8 reduce.10
  37.0 0.9 reshape.289
  37.8 5.5 %all-to-all-start.2 = ((bf16[32,2,2048]{2,1,0:T(2,128)(2,1)}), bf16[32,2,2048]{2,1,0:T(2,128)(2,1)S(1)}, u32[]{:S(2)}, u32[]{:S(2)}) async-start(bf16[32,2,2048]{2,1,0:T(2,128)(2,1)} %reshape.289), calls=%async_computation.2 | async-start | bytes 524288 | tf_op jit(solution)/shard_map/all_to_all | solution.py:118
  43.4 0.3 convolution_bitcast_fusion.1
  43.6 8.8 %all-to-all-done.2 = bf16[32,2,2048]{2,1,0:T(2,128)(2,1)S(1)} async-done(((bf16[32,2,2048]{2,1,0:T(2,128)(2,1)}), bf16[32,2,2048]{2,1,0:T(2,128)(2,1)S(1)}, u32[]{:S(2)}, u32[]{:S(2)}) %all-to-all-start.2) | async-done | bytes 262176 | tf_op jit(solution)/shard_map/all_to_all | solution.py:118
  52.4 0.3 reshape.290
  52.7 0.3 copy.64
  53.0 0.6 gather_fusion.2
  53.7 1.0 %fusion.34 = (f32[6,8,4]{2,1,0:T(8,128)S(1)}, f32[6,8,4,128]{3,2,1,0:T(4,128)S(1)}) fusion(bf16[6,8,4,128]{3,2,1,0:T(4,128)(2,1)S(1)} %gather.20, pred[6]{0:T(512)(128)(4,1)S(1)} %get-tuple-element.7, pred[6,128]{1,0:T(8,128)(4,1)S(1)} %add_compare_fusion, bf16[6,128,1024]{2,1,0:T(8,128)(2,1)S(1)} %copy-done), kind=kOutput, calls=%fused_computation.72 | convolution fusion | flops 6389568 | bytes 1721862 | tf_op jit(solution)/shard_map/sgqd,stgd->sgqt/dot_general | solution.py:63
  55.1 0.6 fusion
  55.7 0.3 fusion.24
  56.1 0.5 fusion.25
  56.8 0.6 copy.34
  57.3 15.3 %all_to_all.46 = f32[32,1,4161]{2,1,0:T(1,128)S(1)} all-to-all(f32[32,1,4161]{2,1,0:T(1,128)S(1)} %copy.34), channel_id=1, replica_groups=mesh['req'=32,'kv'=8] {'req'}, dimensions={0} | all-to-all | bytes 1065216 | tf_op jit(solution)/shard_map/all_to_all | solution.py:38
  73.6 0.6 convolution_bitcast_fusion
  74.4 12.1 %all_to_all.47 = f32[8,1,4160]{2,1,0:T(1,128)S(1)} all-to-all(f32[8,1,4160]{2,1,0:T(1,128)S(1)} %copy.35), channel_id=1, replica_groups=mesh['req'=32,'kv'=8] {'kv'}, dimensions={0} | all-to-all | bytes 266240 | tf_op jit(solution)/shard_map/all_to_all | solution.py:46
  87.1 0.6 divide_convert_fusion
  (42 shorter events, 3.0 us)
Async XLA Ops:
  0.0 53.7 %copy-start = (bf16[6,128,1024]{2,1,0:T(8,128)(2,1)S(1)}, bf16[6,128,1024]{2,1,0:T(8,128)(2,1)}, u32[]{:S(2)}) copy-start(bf16[6,128,1024]{2,1,0:T(8,128)(2,1)} %param.7) | copy-start | bytes 4718596
  4.3 15.5 %all-to-all-start = ((s32[32,1,1]{2,1,0:T(1,128)}), s32[32,1,1]{2,1,0:T(1,128)S(1)}, u32[]{:S(2)}, u32[]{:S(2)}) async-start(s32[32,1,1]{2,1,0:T(1,128)} %copy.29), calls=%async_computation | async-start | bytes 32768 | tf_op jit(solution)/shard_map/all_to_all | solution.py:114
  19.7 15.5 %all-to-all-start.1 = ((bf16[8,2,2048]{2,1,0:T(2,128)(2,1)}), bf16[8,2,2048]{2,1,0:T(2,128)(2,1)S(1)}, u32[]{:S(2)}, u32[]{:S(2)}) async-start(bf16[8,2,2048]{2,1,0:T(2,128)(2,1)} %reshape.287), calls=%async_computation.1 | async-start | bytes 131072 | tf_op jit(solution)/shard_map/all_to_all | solution.py:19
  36.1 7.3 %copy-start.2 = (s32[6]{0:T(128)S(1)}, s32[6]{0:T(128)}, u32[]{:S(2)}) copy-start(s32[6]{0:T(128)} %param.9) | copy-start | bytes 76
  37.8 14.6 %all-to-all-start.2 = ((bf16[32,2,2048]{2,1,0:T(2,128)(2,1)}), bf16[32,2,2048]{2,1,0:T(2,128)(2,1)S(1)}, u32[]{:S(2)}, u32[]{:S(2)}) async-start(bf16[32,2,2048]{2,1,0:T(2,128)(2,1)} %reshape.289), calls=%async_computation.2 | async-start | bytes 524288 | tf_op jit(solution)/shard_map/all_to_all | solution.py:118
  53.0 2.1 %copy-start.1 = (bf16[6,128,1024]{2,1,0:T(8,128)(2,1)S(1)}, bf16[6,128,1024]{2,1,0:T(8,128)(2,1)}, u32[]{:S(2)}) copy-start(bf16[6,128,1024]{2,1,0:T(8,128)(2,1)} %param.8) | copy-start | bytes 4718596
where the time goes:
time: 88.3 us; the launch traced here: 87.7 us
  blocking collectives  27.3 us (31%)
  starting transfers between devices  22.3 us (25%)
  waiting for transfers between devices  19.1 us (22%)
  local copies, waits for them, and re-layouts  7.9 us (9%)
  other arithmetic  7.27 us (8%)
  matrix products  3.5 us (4%)
    all_to_all x1, blocking collectives, in_one_piece(): lax.all_to_all(both, axis, split_axis=split_dim, concat_axis=concat_dim,...  15.3 us
    all_to_all x1, blocking collectives, in_one_piece_2(): lax.all_to_all(both, axis, split_axis=split_dim, concat_axis=concat_dim,...  12.1 us
    all_to_all x1, waiting for transfers between devices, on_device(): lax.all_to_all(picked, 'req', split_axis=0, concat_axis=0, tiled=True)  8.81 us
    all_to_all x1, starting transfers between devices, on_device(): lax.all_to_all(wanted.reshape(groups_req, 1), 'req', split_axis=0, concat...  8.59 us
    all_to_all x1, starting transfers between devices, sent_to_all(): return lax.all_to_all(copies, axis, split_axis=0, concat_axis=0, tiled=True)  8.19 us
    all_to_all x1, waiting for transfers between devices, sent_to_all(): return lax.all_to_all(copies, axis, split_axis=0, concat_axis=0, tiled=True)  6.63 us
    all_to_all x1, starting transfers between devices, on_device(): lax.all_to_all(picked, 'req', split_axis=0, concat_axis=0, tiled=True)  5.51 us
    all_to_all x1, waiting for transfers between devices, on_device(): lax.all_to_all(wanted.reshape(groups_req, 1), 'req', split_axis=0, concat...  3.69 us
  transfers between devices with their start and end apart: 3, of which 3 were waited for; matrix products, arithmetic and copies ran while one was open for 5% of the time, Pallas kernels for 0%

commit v1 on v0

v1 whole, which is shorter than its diff:
```python
import functools

import jax
import jax.numpy as jnp
from jax import lax
from jax.experimental import pallas as pl
from jax.experimental.pallas import tpu as pltpu
from jax.sharding import PartitionSpec as P

HQ = 32
HEAD_SIZE = 128
PAGE = 128
SLOTS = 6
SLOT_ROWS = 8
MESSAGE_ROWS = 40
ABSENT = -2048.0
TOP = 32767.0


def iota(shape, dim):
    return lax.broadcasted_iota(jnp.int32, shape, dim)


def spread_kernel(pages, query, out):
    lane = iota((16, 128), 1)
    even = iota((16, 128), 0) % 2 == 0
    first = (lax.axis_index("req") % 16) * SLOT_ROWS
    ids = jnp.zeros((16, 128), jnp.float32)
    for s in range(SLOTS):
        ids = jnp.where(lane == first + s, pages[s].astype(jnp.float32), ids)
    for h in range(HQ):
        head = query[0:1, h * 128 : (h + 1) * 128].astype(jnp.float32)
        block = jnp.where(even, jnp.broadcast_to(head, (16, 128)), ids)
        out[16 * h : 16 * h + 16, :] = block.astype(jnp.bfloat16)


def select_kernel(recv, out, member):
    rows = recv[...]
    group, plane = lax.axis_index("req"), lax.axis_index("kv")
    at, half = iota((8, 512), 1), iota((8, 512), 0)
    source = at // 2
    pick = (at % 2 == 1) & (source % 8 == plane) & (source // 128 == half)
    ids = jnp.dot(pick.astype(jnp.bfloat16), rows, preferred_element_type=jnp.float32)
    ids = ids.astype(jnp.int32)
    lane = iota((1, 128), 1)
    spots = []
    for n in range(2):
        wanted = ids[n : n + 1, :]
        hot = iota((512, 128), 0) == jnp.broadcast_to(2 * wanted, (512, 128))
        hot = hot.astype(jnp.float32).astype(jnp.bfloat16)
        got = lax.dot_general(
            hot, rows, (((0,), (0,)), ((), ())), preferred_element_type=jnp.float32
        )
        out[128 * n : 128 * n + 128, :] = got.astype(jnp.bfloat16)
        mine = (wanted // 8 == group) & (lane % 8 < SLOTS)
        spots.append(jnp.where(mine, wanted % 8 + 1, 0).astype(jnp.float32))
    dev, lanes = iota((32, 128), 0), iota((32, 128), 1)
    both = jnp.where(dev < 16, spots[0], spots[1])
    own = jnp.where(lanes // 8 == dev % 16, both, 0.0)
    place = jnp.sum(own, axis=1, keepdims=True) - 1.0
    member[...] = jnp.broadcast_to(place, (32, 128))


def coded(out_rows, lse):
    rows = out_rows.shape[0]
    largest = jnp.max(jnp.abs(out_rows), axis=1, keepdims=True)
    power = jnp.ceil(jnp.log2(jnp.maximum(largest, 1e-30)))
    whole = jnp.round(out_rows * (jnp.exp2(-power) * TOP)).astype(jnp.int32).astype(jnp.int16)
    coarse = jnp.round(lse * 16.0)
    fine = jnp.round((lse - coarse * 0.0625) * 524288.0)
    lane = iota((rows, 128), 1)
    stats = jnp.where(lane == 0, coarse, jnp.where(lane == 1, fine, power))
    return whole, jnp.where(lane < 3, stats, 0.0)


def attend_kernel(pages, numbers, lengths, recv, keys, values, out):
    r, c = iota((SLOTS * HQ, 256), 0), iota((SLOTS * HQ, 256), 1)
    order = (c == (r % HQ) * SLOT_ROWS + r // HQ).astype(jnp.float32).astype(jnp.bfloat16)
    query = jnp.dot(order, recv[...], preferred_element_type=jnp.float32)
    upper = iota((8, 128), 0) < 4
    lane = iota((HQ, 128), 1)
    scores = []
    for s in range(SLOTS):
        parts = []
        for i in range(4):
            q = query[s * HQ + 8 * i : s * HQ + 8 * i + 8, :]
            pair = jnp.concatenate([jnp.where(upper, q, 0.0), jnp.where(upper, 0.0, q)], axis=1)
            parts.append(
                lax.dot_general(
                    pair.astype(jnp.bfloat16),
                    keys[s, :, 256 * i : 256 * i + 256],
                    (((1,), (1,)), ((), ())),
                    preferred_element_type=jnp.float32,
                )
            )
        full = jnp.concatenate(parts, axis=0) * HEAD_SIZE**-0.5
        limit = lengths[pages[s]] - numbers[s] * PAGE
        scores.append(jnp.where(lane < limit, full, -1e30))
    scores = jnp.concatenate(scores, axis=0)
    top = jnp.max(scores, axis=1, keepdims=True)
    weights = jnp.exp(scores - top)
    total = jnp.sum(weights, axis=1, keepdims=True)
    rounded = weights.astype(jnp.bfloat16)
    outs = []
    for s in range(SLOTS):
        for i in range(4):
            both = jnp.dot(
                rounded[s * HQ + 8 * i : s * HQ + 8 * i + 8, :],
                values[s, :, 256 * i : 256 * i + 256],
                preferred_element_type=jnp.float32,
            )
            outs.append(jnp.where(upper, both[:, :128], both[:, 128:]))
    outs = jnp.concatenate(outs, axis=0) / total
    whole, stats = coded(outs, top + jnp.log(total))
    out[...] = jnp.zeros(out.shape, jnp.int16)
    for s in range(SLOTS):
        target = pages[s] // 8
        out[target, 0:HQ, :] = whole[s * HQ : s * HQ + HQ, :]
        turned = jnp.transpose(stats[s * HQ : s * HQ + HQ, :])
        tile = jnp.concatenate([turned[0:8, :], jnp.zeros((8, 96), jnp.float32)], axis=1)
        out[target, HQ:MESSAGE_ROWS, :] = tile.astype(jnp.int32).astype(jnp.int16)


def statistics(recv, count):
    tiles = recv[:, HQ:MESSAGE_ROWS, :].astype(jnp.int32).astype(jnp.float32)
    coarse, fine, power = tiles[:, 0, :], tiles[:, 1, :], tiles[:, 2, :]
    lse = coarse * 0.0625 + fine * (1.0 / 524288.0)
    return lse, jnp.exp2(power) * (1.0 / TOP)


def merge_kernel(recv, member, out):
    place = member[...]
    lse, unit = statistics(recv, 32)
    tops, sums = [], []
    peak = jnp.zeros((32, 128), jnp.float32)
    for j in range(8):
        top = jnp.max(jnp.where(place == j, lse, ABSENT), axis=0, keepdims=True)
        tops.append(top)
        peak = jnp.where(place == j, top, peak)
    weight = jnp.where(place >= 0.0, jnp.exp(lse - peak), 0.0)
    total = jnp.ones((32, 128), jnp.float32)
    for j in range(8):
        add = jnp.sum(jnp.where(place == j, weight, 0.0), axis=0, keepdims=True)
        sums.append(add)
        total = jnp.where(place == j, add, total)
    factor = jnp.transpose(weight / total * unit)[0:HQ, :]
    accs = [jnp.zeros((HQ, 128), jnp.float32) for _ in range(8)]
    for g in range(32):
        row = recv[g, 0:HQ, :].astype(jnp.int32).astype(jnp.float32)
        row = row * jnp.broadcast_to(factor[:, g : g + 1], (HQ, 128))
        at = jnp.broadcast_to(place[g : g + 1, :], (HQ, 128))
        accs = [acc + jnp.where(at == j, row, 0.0) for j, acc in enumerate(accs)]
    lses = [
        jnp.where(add > 0.0, top + jnp.log(jnp.maximum(add, 1e-30)), ABSENT)
        for top, add in zip(tops, sums)
    ]
    spare = jnp.zeros((8, 128), jnp.float32)
    for j in range(8):
        largest = jnp.max(jnp.abs(accs[j]), axis=1, keepdims=True)
        power = jnp.ceil(jnp.log2(jnp.maximum(largest, 1e-30)))
        whole = jnp.round(accs[j] * (jnp.exp2(-power) * TOP)).astype(jnp.int32)
        out[j, 0:HQ, :] = whole.astype(jnp.int16)
        coarse = jnp.round(lses[j] * 16.0)
        fine = jnp.round((lses[j] - coarse * 0.0625) * 524288.0)
        turned = jnp.transpose(jnp.broadcast_to(power, (HQ, 128)))[0:8, :]
        turned = jnp.concatenate([turned, jnp.zeros((8, 96), jnp.float32)], axis=1)
        row = iota((8, 128), 0)
        tile = jnp.where(row == 0, coarse, jnp.where(row == 1, fine, turned))
        tile = jnp.where(row < 3, tile, spare)
        out[j, HQ:MESSAGE_ROWS, :] = tile.astype(jnp.int32).astype(jnp.int16)


def finish_kernel(recv, out):
    lse, unit = statistics(recv, 8)
    top = jnp.max(lse, axis=0, keepdims=True)
    weight = jnp.exp(lse - top)
    total = jnp.sum(weight, axis=0, keepdims=True)
    factor = jnp.transpose(weight / total * unit)[0:HQ, :]
    acc = jnp.zeros((HQ, 128), jnp.float32)
    for k in range(8):
        row = recv[k, 0:HQ, :].astype(jnp.int32).astype(jnp.float32)
        acc = acc + row * jnp.broadcast_to(factor[:, k : k + 1], (HQ, 128))
    for h in range(HQ):
        out[0:1, 128 * h : 128 * h + 128] = acc[h : h + 1, :].astype(jnp.bfloat16)


VMEM = pl.BlockSpec(memory_space=pltpu.VMEM)
SMEM = pl.BlockSpec(memory_space=pltpu.SMEM)


def kernel_call(kernel, shapes, specs, name):
    return pl.pallas_call(
        kernel,
        out_shape=shapes,
        in_specs=specs,
        out_specs=jax.tree.map(lambda _: VMEM, shapes),
        name=name,
        compiler_params=pltpu.CompilerParams(vmem_limit_bytes=32 * 1024 * 1024),
    )


def on_device(queries, paged_key_cache, paged_value_cache, page_request, page_number, lengths):
    shape = jax.ShapeDtypeStruct
    sent = kernel_call(spread_kernel, shape((512, 128), jnp.bfloat16), [SMEM, VMEM], "spread")(
        page_request, queries
    )
    heads = lax.all_to_all(sent, ("req", "kv"), 0, 0, tiled=True)
    picked, member = kernel_call(
        select_kernel,
        (shape((256, 128), jnp.bfloat16), shape((32, 128), jnp.float32)),
        [VMEM],
        "select",
    )(heads)
    wanted = lax.all_to_all(picked, "req", 0, 0, tiled=True)
    partial = kernel_call(
        attend_kernel,
        shape((32, MESSAGE_ROWS, 128), jnp.int16),
        [SMEM, SMEM, SMEM, VMEM, VMEM, VMEM],
        "attend",
    )(page_request, page_number, lengths, wanted, paged_key_cache, paged_value_cache)
    partial = lax.all_to_all(partial, "req", 0, 0, tiled=True)
    merged = kernel_call(
        merge_kernel, shape((8, MESSAGE_ROWS, 128), jnp.int16), [VMEM, VMEM], "merge"
    )(partial, member)
    merged = lax.all_to_all(merged, "kv", 0, 0, tiled=True)
    return kernel_call(finish_kernel, shape((1, 4096), jnp.bfloat16), [VMEM], "finish")(merged)


def solution(mesh):
    placed = (
        P(("req", "kv"), None),
        P(("req", "kv"), None, None),
        P(("req", "kv"), None, None),
        P(("req", "kv")),
        P(("req", "kv")),
        P(),
    )
    return jax.shard_map(
        on_device, mesh=mesh, in_specs=placed, out_specs=P(("req", "kv"), None), check_vma=False
    )
```

time: 88.3 us -> 73.6 us (0.83)
  blocking collectives: 27.3 us -> 62.8 us
  starting transfers between devices: 22.3 us -> 0 us
  waiting for transfers between devices: 19.1 us -> 0 us
  other arithmetic: 7.27 us -> 0 us
  Pallas kernels: 0 us -> 4.22 us
  matrix products: 3.5 us -> 0 us
  local copies, waits for them, and re-layouts: 7.9 us -> 6.17 us
    all_to_all x2 -> x4, blocking collectives: 27.3 us -> 62.8 us  [the longest x1 28.5 us: on_device(): heads = lax.all_to_all(sent, ('req', 'kv'), 0, 0, tiled=True)]
    all_to_all x3 -> x0, starting transfers between devices: 22.3 us -> none  [the longest x1 8.59 us: on_device(): lax.all_to_all(wanted.reshape(groups_req, 1), 'req', split_axis=0, concat...]
    all_to_all x3 -> x0, waiting for transfers between devices: 19.1 us -> none  [the longest x1 8.81 us: on_device(): lax.all_to_all(picked, 'req', split_axis=0, concat_axis=0, tiled=True)]
    pallas_call x0 -> x5, Pallas kernels: none -> 4.22 us  [the longest x1 1.55 us: on_device(): kernel_call(attend_kernel, shape((32, MESSAGE_ROWS, 128), jnp.int16), [SM...]
    unnamed x13 -> x14, local copies, waits for them, and re-layouts: 2.28 us -> 6.17 us
    dot_general x7 -> x0, matrix products: 3.5 us -> none  [the longest x1 1.02 us: page_attention(): jnp.einsum('sgqd,stgd->sgqt', query_half, key_half, preferred_element_typ...]
    gather x4 -> x0, local copies, waits for them, and re-layouts: 2.69 us -> none  [the longest x1 1.33 us: on_device(): limits = jnp.take(lengths, page_request)]
    select_n x6 -> x0, other arithmetic: 2.31 us -> none  [the longest x2 1.46 us: on_device(): limits = jnp.take(lengths, page_request)]
  transfers between devices with their start and end apart: 3 -> 0, of which waited for: 3 -> 0; matrix products, arithmetic and copies ran while one was open for 5% -> 0% of each run, Pallas kernels for 0% -> 0%
where the time goes in v1:
time: 73.6 us; the launch traced here: 73.2 us
  blocking collectives  62.8 us (85%)
  local copies, waits for them, and re-layouts  6.17 us (8%)
  Pallas kernels  4.22 us (6%)
    all_to_all x1, blocking collectives, on_device(): heads = lax.all_to_all(sent, ('req', 'kv'), 0, 0, tiled=True)  28.5 us
    all_to_all x1, blocking collectives, on_device(): partial = lax.all_to_all(partial, 'req', 0, 0, tiled=True)  13.1 us
    all_to_all x1, blocking collectives, on_device(): wanted = lax.all_to_all(picked, 'req', 0, 0, tiled=True)  11.1 us
    all_to_all x1, blocking collectives, on_device(): merged = lax.all_to_all(merged, 'kv', 0, 0, tiled=True)  10.1 us
    unnamed x14, local copies, waits for them, and re-layouts  6.17 us
    pallas_call x1, Pallas kernels, on_device(): kernel_call(attend_kernel, shape((32, MESSAGE_ROWS, 128), jnp.int16), [SM...  1.55 us

profile of v1, /device:TPU:1, one launch (start us, length us, event | category | flops | bytes accessed | tf_op | source)
XLA Modules:
  0.0 73.2 jit_solution(15362646563286763282)
XLA Ops:
  0.0 0.0 copy-start.2
  0.0 0.7 copy-done.2
  0.7 0.0 copy-start.3
  0.7 0.7 copy-done.3
  1.4 0.6 spread.1
  2.0 28.5 %all_to_all.32 = bf16[256,2,128]{2,1,0:T(2,128)(2,1)S(1)} all-to-all(bf16[256,2,128]{2,1,0:T(2,128)(2,1)S(1)} %bitcast.5), channel_id=1, replica_groups=mesh['req'=32,'kv'=8] {'req','kv'}, dimensions={0} | all-to-all | bytes 262144 | tf_op jit(solution)/shard_map/all_to_all | solution.py:207
  30.5 0.4 select.1
  30.9 11.1 %all_to_all.33 = bf16[32,8,128]{2,1,0:T(8,128)(2,1)S(1)} all-to-all(bf16[32,8,128]{2,1,0:T(8,128)(2,1)S(1)} %bitcast.7), channel_id=1, replica_groups=mesh['req'=32,'kv'=8] {'req'}, dimensions={0} | all-to-all | bytes 131072 | tf_op jit(solution)/shard_map/all_to_all | solution.py:214
  41.9 0.0 copy-start
  41.9 1.4 %copy-done = bf16[6,128,1024]{2,1,0:T(8,128)(2,1)S(1)} copy-done((bf16[6,128,1024]{2,1,0:T(8,128)(2,1)S(1)}, bf16[6,128,1024]{2,1,0:T(8,128)(2,1)}, u32[]{:S(2)}) %copy-start) | copy-done | bytes 1572888
  43.3 0.0 copy-start.1
  43.3 1.4 %copy-done.1 = bf16[6,128,1024]{2,1,0:T(8,128)(2,1)S(1)} copy-done((bf16[6,128,1024]{2,1,0:T(8,128)(2,1)S(1)}, bf16[6,128,1024]{2,1,0:T(8,128)(2,1)}, u32[]{:S(2)}) %copy-start.1) | copy-done | bytes 1572888
  44.8 0.0 copy-start.4
  44.8 0.7 copy-done.4
  45.4 0.0 copy-start.5
  45.4 0.7 copy-done.5
  46.1 0.0 copy-start.6
  46.1 0.7 copy-done.6
  46.7 1.6 %attend.1 = s16[32,40,128]{2,1,0:T(8,128)(2,1)S(1)} custom-call(s32[6]{0:T(128)S(1)} %copy-done.4, s32[6]{0:T(128)S(1)} %copy-done.6, s32[256]{0:T(256)S(1)} %copy-done.5, bf16[256,128]{1,0:T(8,128)(2,1)S(1)} %bitcast.6, bf16[6,128,1024]{2,1,0:T(8,128)(2,1)S(1)} %copy-done, bf16[6,128,1024]{2,1,0:T(8,128)(2,1)S(1)} %copy-done.1), custom_call_target="tpu_custom_call" | custom-call | tf_op jit(solution)/shard_map/attend/pallas_call | solution.py:215
  48.3 13.1 %all_to_all.34.recv = s16[32,40,128]{2,1,0:T(8,128)(2,1)S(1)} all-to-all(s16[32,40,128]{2,1,0:T(8,128)(2,1)S(1)} %attend.1), channel_id=1, replica_groups=mesh['req'=32,'kv'=8] {'req'}, dimensions={0} | all-to-all | bytes 655360 | tf_op jit(solution)/shard_map/all_to_all | solution.py:221
  61.4 0.8 %merge.1 = s16[8,40,128]{2,1,0:T(8,128)(2,1)S(1)} custom-call(s16[32,40,128]{2,1,0:T(8,128)(2,1)S(1)} %all_to_all.34.recv, f32[32,128]{1,0:T(8,128)S(1)} %get-tuple-element.8.member), custom_call_target="tpu_custom_call" | custom-call | tf_op jit(solution)/shard_map/merge/pallas_call | solution.py:222
  62.3 10.1 %all_to_all.35.recv = s16[8,40,128]{2,1,0:T(8,128)(2,1)S(1)} all-to-all(s16[8,40,128]{2,1,0:T(8,128)(2,1)S(1)} %merge.1), channel_id=1, replica_groups=mesh['req'=32,'kv'=8] {'kv'}, dimensions={0} | all-to-all | bytes 163840 | tf_op jit(solution)/shard_map/all_to_all | solution.py:225
  72.4 0.8 %finish.1 = bf16[1,4096]{1,0:T(2,128)(2,1)} custom-call(s16[8,40,128]{2,1,0:T(8,128)(2,1)S(1)} %all_to_all.35.recv), custom_call_target="tpu_custom_call" | custom-call | tf_op jit(solution)/shard_map/finish/pallas_call | solution.py:226
Async XLA Ops:
  0.0 0.7 copy-start.2
  0.7 0.7 copy-start.3
  41.9 1.4 %copy-start = (bf16[6,128,1024]{2,1,0:T(8,128)(2,1)S(1)}, bf16[6,128,1024]{2,1,0:T(8,128)(2,1)}, u32[]{:S(2)}) copy-start(bf16[6,128,1024]{2,1,0:T(8,128)(2,1)} %keys.1) | copy-start | bytes 4718596
  43.3 1.4 %copy-start.1 = (bf16[6,128,1024]{2,1,0:T(8,128)(2,1)S(1)}, bf16[6,128,1024]{2,1,0:T(8,128)(2,1)}, u32[]{:S(2)}) copy-start(bf16[6,128,1024]{2,1,0:T(8,128)(2,1)} %values.1) | copy-start | bytes 4718596
  44.8 0.7 copy-start.4
  45.4 0.7 copy-start.5
  46.1 0.7 copy-start.6

commit v2 on v1

--- a/solution.py
+++ b/solution.py
@@ -1,5 +1,3 @@
-import functools
-
 import jax
 import jax.numpy as jnp
 from jax import lax
@@ -21,7 +19,13 @@
     return lax.broadcasted_iota(jnp.int32, shape, dim)
 
 
-def spread_kernel(pages, query, out):
+def spread_kernel(pages_in, query_in, out, pages, query, sems):
+    first_copy = pltpu.make_async_copy(pages_in, pages, sems.at[0])
+    second_copy = pltpu.make_async_copy(query_in, query, sems.at[1])
+    first_copy.start()
+    second_copy.start()
+    first_copy.wait()
+    second_copy.wait()
     lane = iota((16, 128), 1)
     even = iota((16, 128), 0) % 2 == 0
     first = (lax.axis_index("req") % 16) * SLOT_ROWS
@@ -94,8 +98,7 @@
                 )
             )
         full = jnp.concatenate(parts, axis=0) * HEAD_SIZE**-0.5
-        limit = lengths[pages[s]] - numbers[s] * PAGE
-        scores.append(jnp.where(lane < limit, full, -1e30))
+        scores.append(jnp.where(lane < lengths[pages[s]] - numbers[s] * PAGE, full, -1e30))
     scores = jnp.concatenate(scores, axis=0)
     top = jnp.max(scores, axis=1, keepdims=True)
     weights = jnp.exp(scores - top)
@@ -186,23 +189,37 @@
 
 VMEM = pl.BlockSpec(memory_space=pltpu.VMEM)
 SMEM = pl.BlockSpec(memory_space=pltpu.SMEM)
-
-
-def kernel_call(kernel, shapes, specs, name):
+HBM = pl.BlockSpec(memory_space=pltpu.MemorySpace.HBM)
+
+
+def kernel_call(kernel, shapes, in_specs, name, out_specs=None, scratch=(), flops=None):
     return pl.pallas_call(
         kernel,
         out_shape=shapes,
-        in_specs=specs,
-        out_specs=jax.tree.map(lambda _: VMEM, shapes),
+        in_specs=in_specs,
+        out_specs=jax.tree.map(lambda _: VMEM, shapes) if out_specs is None else out_specs,
+        scratch_shapes=scratch,
         name=name,
+        cost_estimate=flops and pl.CostEstimate(flops, 0, 0),
         compiler_params=pltpu.CompilerParams(vmem_limit_bytes=32 * 1024 * 1024),
     )
 
 
 def on_device(queries, paged_key_cache, paged_value_cache, page_request, page_number, lengths):
     shape = jax.ShapeDtypeStruct
-    sent = kernel_call(spread_kernel, shape((512, 128), jnp.bfloat16), [SMEM, VMEM], "spread")(
-        page_request, queries
+    sent = kernel_call(
+        spread_kernel,
+        shape((512, 128), jnp.bfloat16),
+        [HBM, HBM],
+        "spread",
+        scratch=[
+            pltpu.SMEM((SLOTS,), jnp.int32),
+            pltpu.VMEM((1, HQ * HEAD_SIZE), jnp.bfloat16),
+            pltpu.SemaphoreType.DMA((2,)),
+        ],
+    )(
+        pltpu.with_memory_space_constraint(page_request, pltpu.MemorySpace.HBM),
+        pltpu.with_memory_space_constraint(queries, pltpu.MemorySpace.HBM),
     )
     heads = lax.all_to_all(sent, ("req", "kv"), 0, 0, tiled=True)
     picked, member = kernel_call(
@@ -210,6 +227,7 @@
         (shape((256, 128), jnp.bfloat16), shape((32, 128), jnp.float32)),
         [VMEM],
         "select",
+        flops=10**10,
     )(heads)
     wanted = lax.all_to_all(picked, "req", 0, 0, tiled=True)
     partial = kernel_call(

time: 73.6 us -> 67.7 us (0.920)
  local copies, waits for them, and re-layouts: 6.17 us -> 0.02 us
    unnamed x14 -> x10, local copies, waits for them, and re-layouts: 6.17 us -> 0.02 us
where the time goes in v2:
time: 67.7 us; the launch traced here: 67.4 us
  blocking collectives  62.9 us (93%)
  Pallas kernels  4.42 us (7%)
    all_to_all x1, blocking collectives, on_device(): heads = lax.all_to_all(sent, ('req', 'kv'), 0, 0, tiled=True)  28.5 us
    all_to_all x1, blocking collectives, on_device(): partial = lax.all_to_all(partial, 'req', 0, 0, tiled=True)  13.1 us
    all_to_all x1, blocking collectives, on_device(): wanted = lax.all_to_all(picked, 'req', 0, 0, tiled=True)  11.2 us
    all_to_all x1, blocking collectives, on_device(): merged = lax.all_to_all(merged, 'kv', 0, 0, tiled=True)  10.1 us
    pallas_call x1, Pallas kernels, on_device(): kernel_call(attend_kernel, shape((32, MESSAGE_ROWS, 128), jnp.int16), [SM...  1.55 us

profile of v2, /device:TPU:1, one launch (start us, length us, event | category | flops | bytes accessed | tf_op | source)
XLA Modules:
  0.0 67.4 jit_solution(13343454169052522960)
XLA Ops:
  0.0 0.8 %spread.1 = bf16[512,128]{1,0:T(8,128)(2,1)S(1)} custom-call(s32[6]{0:T(128)} %pages.1, bf16[1,4096]{1,0:T(2,128)(2,1)} %query_in.1), custom_call_target="tpu_custom_call" | custom-call | tf_op jit(solution)/shard_map/spread/pallas_call | solution.py:210
  0.8 28.5 %all_to_all.32 = bf16[256,2,128]{2,1,0:T(2,128)(2,1)S(1)} all-to-all(bf16[256,2,128]{2,1,0:T(2,128)(2,1)S(1)} %bitcast.4), channel_id=1, replica_groups=mesh['req'=32,'kv'=8] {'req','kv'}, dimensions={0} | all-to-all | bytes 262144 | tf_op jit(solution)/shard_map/all_to_all | solution.py:224
  29.3 0.0 copy-start
  29.3 0.0 copy-start.1
  29.3 0.0 copy-start.2
  29.3 0.0 copy-start.3
  29.3 0.0 copy-start.4
  29.3 0.4 select.1
  29.7 11.2 %all_to_all.33 = bf16[32,8,128]{2,1,0:T(8,128)(2,1)S(1)} all-to-all(bf16[32,8,128]{2,1,0:T(8,128)(2,1)S(1)} %bitcast.7), channel_id=1, replica_groups=mesh['req'=32,'kv'=8] {'req'}, dimensions={0} | all-to-all | bytes 131072 | tf_op jit(solution)/shard_map/all_to_all | solution.py:232
  40.9 0.0 copy-done
  40.9 0.0 copy-done.1
  40.9 0.0 copy-done.2
  40.9 0.0 copy-done.3
  40.9 0.0 copy-done.4
  40.9 1.6 %attend.1 = s16[32,40,128]{2,1,0:T(8,128)(2,1)S(1)} custom-call(s32[6]{0:T(128)S(1)} %copy-done.2, s32[6]{0:T(128)S(1)} %copy-done.4, s32[256]{0:T(256)S(1)} %copy-done.3, bf16[256,128]{1,0:T(8,128)(2,1)S(1)} %bitcast.5, bf16[6,128,1024]{2,1,0:T(8,128)(2,1)S(1)} %copy-done, bf16[6,128,1024]{2,1,0:T(8,128)(2,1)S(1)} %copy-done.1), custom_call_target="tpu_custom_call" | custom-call | tf_op jit(solution)/shard_map/attend/pallas_call | solution.py:233
  42.5 13.1 %all_to_all.34.recv = s16[32,40,128]{2,1,0:T(8,128)(2,1)S(1)} all-to-all(s16[32,40,128]{2,1,0:T(8,128)(2,1)S(1)} %attend.1), channel_id=1, replica_groups=mesh['req'=32,'kv'=8] {'req'}, dimensions={0} | all-to-all | bytes 655360 | tf_op jit(solution)/shard_map/all_to_all | solution.py:239
  55.6 0.8 %merge.1 = s16[8,40,128]{2,1,0:T(8,128)(2,1)S(1)} custom-call(s16[32,40,128]{2,1,0:T(8,128)(2,1)S(1)} %all_to_all.34.recv, f32[32,128]{1,0:T(8,128)S(1)} %get-tuple-element.8.member), custom_call_target="tpu_custom_call" | custom-call | tf_op jit(solution)/shard_map/merge/pallas_call | solution.py:240
  56.5 10.1 %all_to_all.35.recv = s16[8,40,128]{2,1,0:T(8,128)(2,1)S(1)} all-to-all(s16[8,40,128]{2,1,0:T(8,128)(2,1)S(1)} %merge.1), channel_id=1, replica_groups=mesh['req'=32,'kv'=8] {'kv'}, dimensions={0} | all-to-all | bytes 163840 | tf_op jit(solution)/shard_map/all_to_all | solution.py:243
  66.6 0.8 %finish.1 = bf16[1,4096]{1,0:T(2,128)(2,1)} custom-call(s16[8,40,128]{2,1,0:T(8,128)(2,1)S(1)} %all_to_all.35.recv), custom_call_target="tpu_custom_call" | custom-call | tf_op jit(solution)/shard_map/finish/pallas_call | solution.py:244
Async XLA Ops:
  29.3 11.6 %copy-start = (bf16[6,128,1024]{2,1,0:T(8,128)(2,1)S(1)}, bf16[6,128,1024]{2,1,0:T(8,128)(2,1)}, u32[]{:S(2)}) copy-start(bf16[6,128,1024]{2,1,0:T(8,128)(2,1)} %keys.1) | copy-start | bytes 4718596
  29.3 11.6 %copy-start.1 = (bf16[6,128,1024]{2,1,0:T(8,128)(2,1)S(1)}, bf16[6,128,1024]{2,1,0:T(8,128)(2,1)}, u32[]{:S(2)}) copy-start(bf16[6,128,1024]{2,1,0:T(8,128)(2,1)} %values.1) | copy-start | bytes 4718596
  29.3 11.6 %copy-start.2 = (s32[6]{0:T(128)S(1)}, s32[6]{0:T(128)}, u32[]{:S(2)}) copy-start(s32[6]{0:T(128)} %pages.1) | copy-start | bytes 76
  29.3 11.6 %copy-start.3 = (s32[256]{0:T(256)S(1)}, s32[256]{0:T(256)}, u32[]{:S(2)}) copy-start(s32[256]{0:T(256)} %lengths.1) | copy-start | bytes 3076
  29.3 11.6 %copy-start.4 = (s32[6]{0:T(128)S(1)}, s32[6]{0:T(128)}, u32[]{:S(2)}) copy-start(s32[6]{0:T(128)} %numbers.1) | copy-start | bytes 76

commit v3 on v2

v3 whole, which is shorter than its diff:
```python
import jax
import jax.numpy as jnp
from jax import lax
from jax.experimental import pallas as pl
from jax.experimental.pallas import tpu as pltpu
from jax.sharding import PartitionSpec as P

HQ = 32
HEAD_SIZE = 128
PAGE = 128
SLOTS = 6
SLOT_ROWS = 8
MESSAGE_ROWS = 40
ABSENT = -2048.0
TOP = 32767.0


def iota(shape, dim):
    return lax.broadcasted_iota(jnp.int32, shape, dim)


def spread_kernel(pages_in, query_in, out, pages, query, sems):
    first_copy = pltpu.make_async_copy(pages_in, pages, sems.at[0])
    second_copy = pltpu.make_async_copy(query_in, query, sems.at[1])
    first_copy.start()
    second_copy.start()
    first_copy.wait()
    second_copy.wait()
    lane = iota((16, 128), 1)
    even = iota((16, 128), 0) % 2 == 0
    first = (lax.axis_index("req") % 16) * SLOT_ROWS
    ids = jnp.zeros((16, 128), jnp.float32)
    for s in range(SLOTS):
        ids = jnp.where(lane == first + s, pages[s].astype(jnp.float32), ids)
    for h in range(HQ):
        head = query[0:1, h * 128 : (h + 1) * 128].astype(jnp.float32)
        block = jnp.where(even, jnp.broadcast_to(head, (16, 128)), ids)
        out[16 * h : 16 * h + 16, :] = block.astype(jnp.bfloat16)


def select_kernel(recv, out, member):
    rows = recv[...]
    group, plane = lax.axis_index("req"), lax.axis_index("kv")
    at, half = iota((8, 512), 1), iota((8, 512), 0)
    source = at // 2
    pick = (at % 2 == 1) & (source % 8 == plane) & (source // 128 == half)
    ids = jnp.dot(pick.astype(jnp.bfloat16), rows, preferred_element_type=jnp.float32)
    ids = ids.astype(jnp.int32)
    lane = iota((1, 128), 1)
    spots = []
    for n in range(2):
        wanted = ids[n : n + 1, :]
        hot = iota((512, 128), 0) == jnp.broadcast_to(2 * wanted, (512, 128))
        hot = hot.astype(jnp.float32).astype(jnp.bfloat16)
        got = lax.dot_general(
            hot, rows, (((0,), (0,)), ((), ())), preferred_element_type=jnp.float32
        )
        out[128 * n : 128 * n + 128, :] = got.astype(jnp.bfloat16)
        mine = (wanted // 8 == group) & (lane % 8 < SLOTS)
        spots.append(jnp.where(mine, wanted % 8 + 1, 0).astype(jnp.float32))
    dev, lanes = iota((32, 128), 0), iota((32, 128), 1)
    both = jnp.where(dev < 16, spots[0], spots[1])
    own = jnp.where(lanes // 8 == dev % 16, both, 0.0)
    place = jnp.sum(own, axis=1, keepdims=True) - 1.0
    member[...] = jnp.broadcast_to(place, (32, 128))


def attend_kernel(pages, numbers, lengths, recv, keys, values, out):
    whose, counts = pages[...], lengths[...].astype(jnp.float32)
    before = numbers[...].astype(jnp.float32) * PAGE
    request = iota(counts.shape, 1)
    limits, targets = [], []
    for s in range(SLOTS):
        own = request == whose[:, s : s + 1]
        count = jnp.sum(jnp.where(own, counts, 0.0), axis=1, keepdims=True)
        limits.append(jnp.broadcast_to(count - before[:, s : s + 1], (8, 128)))
        group = jnp.max(whose[:, s : s + 1].astype(jnp.float32)).astype(jnp.int32)
        targets.append(lax.shift_right_logical(group, 3))
    rows = SLOTS * HQ
    r, c = iota((rows, 256), 0), iota((rows, 256), 1)
    slot, head = r // 64 * 2 + r // 8 % 2, r // 16 % 4 * 8 + r % 8
    order = (c == head * SLOT_ROWS + slot).astype(jnp.float32).astype(jnp.bfloat16)
    query = jnp.dot(order, recv[...], preferred_element_type=jnp.float32)
    upper = iota((rows, 128), 0) % 8 < 4
    both = jnp.concatenate([jnp.where(upper, query, 0.0), jnp.where(upper, 0.0, query)], axis=1)
    both = both.astype(jnp.bfloat16)
    lane = iota((8, 128), 1).astype(jnp.float32)
    scores = []
    for p in range(SLOTS // 2):
        for i in range(4):
            at = 64 * p + 16 * i
            tile = lax.dot_general(
                both[at : at + 16, :],
                keys[2 * p : 2 * p + 2, :, 256 * i : 256 * i + 256].reshape(256, 256),
                (((1,), (1,)), ((), ())),
                preferred_element_type=jnp.float32,
            )
            for n in range(2):
                part = tile[8 * n : 8 * n + 8, 128 * n : 128 * n + 128] * HEAD_SIZE**-0.5
                scores.append(jnp.where(lane < limits[2 * p + n], part, -1e30))
    scores = jnp.concatenate(scores, axis=0)
    top = jnp.max(scores, axis=1, keepdims=True)
    weights = jnp.exp(scores - top)
    total = jnp.sum(weights, axis=1, keepdims=True)
    first = iota((rows, 128), 0) % 16 < 8
    wide = jnp.concatenate([jnp.where(first, weights, 0.0), jnp.where(first, 0.0, weights)], axis=1)
    wide = wide.astype(jnp.bfloat16)
    outs = []
    for p in range(SLOTS // 2):
        for i in range(4):
            at = 64 * p + 16 * i
            tile = jnp.dot(
                wide[at : at + 16, :],
                values[2 * p : 2 * p + 2, :, 256 * i : 256 * i + 256].reshape(256, 256),
                preferred_element_type=jnp.float32,
            )
            outs.append(jnp.where(upper[0:16, :], tile[:, :128], tile[:, 128:]))
    outs = jnp.concatenate(outs, axis=0) / total
    largest = jnp.max(jnp.abs(outs), axis=1, keepdims=True)
    power = jnp.ceil(jnp.log2(jnp.maximum(largest, 1e-30)))
    whole = jnp.round(outs * (jnp.exp2(-power) * TOP)).astype(jnp.int32).astype(jnp.int16)
    lanes = iota((rows, 128), 1)
    stats = jnp.where(lanes == 0, top + jnp.log(total), jnp.where(lanes == 1, power, 0.0))
    out[...] = jnp.zeros(out.shape, jnp.int16)
    for s in range(SLOTS):
        target = targets[s]
        starts = [64 * (s // 2) + 16 * i + 8 * (s % 2) for i in range(4)]
        out[target, 0:HQ, :] = jnp.concatenate([whole[a : a + 8, :] for a in starts], axis=0)
        turned = jnp.transpose(jnp.concatenate([stats[a : a + 8, :] for a in starts], axis=0))
        turned = jnp.concatenate([turned[0:8, :], jnp.zeros((8, 96), jnp.float32)], axis=1)
        out[target, HQ:MESSAGE_ROWS, :] = statistics_tile(turned[0:1, :], turned[1:2, :])


def statistics_tile(lse, power):
    row = iota((8, 128), 0)
    coarse = jnp.round(lse * 16.0)
    fine = jnp.round((lse - coarse * 0.0625) * 524288.0)
    tile = jnp.where(row == 0, coarse, jnp.where(row == 1, fine, jnp.where(row == 2, power, 0.0)))
    return tile.astype(jnp.int32).astype(jnp.int16)


def statistics(recv):
    tiles = recv[:, HQ:MESSAGE_ROWS, :].astype(jnp.int32).astype(jnp.float32)
    return tiles[:, 0, :] * 0.0625 + tiles[:, 1, :] * (1.0 / 524288.0), tiles[:, 2, :]


def merge_kernel(recv, member, out):
    place = member[...]
    lse, power = statistics(recv)
    peak, unit, total = (jnp.zeros((32, 128), jnp.float32) for _ in range(3))
    tops, units, sums = [], [], []
    for j in range(8):
        own = place == j
        tops.append(jnp.max(jnp.where(own, lse, ABSENT), axis=0, keepdims=True))
        units.append(jnp.max(jnp.where(own, power, -110.0), axis=0, keepdims=True))
        peak = jnp.where(own, tops[j], peak)
        unit = jnp.where(own, units[j], unit)
    weight = jnp.where(place >= 0.0, jnp.exp(lse - peak), 0.0)
    for j in range(8):
        own = place == j
        sums.append(jnp.sum(jnp.where(own, weight, 0.0), axis=0, keepdims=True))
        total = jnp.where(own, sums[j], total)
    total = jnp.where(place >= 0.0, total, 1.0)
    factor = jnp.transpose(weight / total * jnp.exp2(power - unit))[0:HQ, :]
    accs = [jnp.zeros((HQ, 128), jnp.float32) for _ in range(8)]
    for g in range(32):
        row = recv[g, 0:HQ, :].astype(jnp.int32).astype(jnp.float32)
        row = row * jnp.broadcast_to(factor[:, g : g + 1], (HQ, 128))
        at = jnp.broadcast_to(place[g : g + 1, :], (HQ, 128))
        accs = [acc + jnp.where(at == j, row, 0.0) for j, acc in enumerate(accs)]
    for j in range(8):
        out[j, 0:HQ, :] = jnp.round(accs[j]).astype(jnp.int32).astype(jnp.int16)
        lse = jnp.where(sums[j] > 0.0, tops[j] + jnp.log(jnp.maximum(sums[j], 1e-30)), ABSENT)
        out[j, HQ:MESSAGE_ROWS, :] = statistics_tile(lse, units[j])


def finish_kernel(recv, out):
    lse, power = statistics(recv)
    weight = jnp.exp(lse - jnp.max(lse, axis=0, keepdims=True))
    total = jnp.sum(weight, axis=0, keepdims=True)
    factor = jnp.transpose(weight / total * (jnp.exp2(power) * (1.0 / TOP)))[0:HQ, :]
    acc = jnp.zeros((HQ, 128), jnp.float32)
    for k in range(8):
        row = recv[k, 0:HQ, :].astype(jnp.int32).astype(jnp.float32)
        acc = acc + row * jnp.broadcast_to(factor[:, k : k + 1], (HQ, 128))
    for h in range(HQ):
        out[0:1, 128 * h : 128 * h + 128] = acc[h : h + 1, :].astype(jnp.bfloat16)


VMEM = pl.BlockSpec(memory_space=pltpu.VMEM)
HBM = pl.BlockSpec(memory_space=pltpu.MemorySpace.HBM)


def kernel_call(kernel, shapes, in_specs, name, scratch=(), flops=None):
    return pl.pallas_call(
        kernel,
        out_shape=shapes,
        in_specs=in_specs,
        out_specs=jax.tree.map(lambda _: VMEM, shapes),
        scratch_shapes=scratch,
        name=name,
        cost_estimate=flops and pl.CostEstimate(flops, 0, 0),
        compiler_params=pltpu.CompilerParams(vmem_limit_bytes=32 * 1024 * 1024),
    )


def on_device(queries, paged_key_cache, paged_value_cache, page_request, page_number, lengths):
    shape = jax.ShapeDtypeStruct
    sent = kernel_call(
        spread_kernel,
        shape((512, 128), jnp.bfloat16),
        [HBM, HBM],
        "spread",
        scratch=[
            pltpu.SMEM((SLOTS,), jnp.int32),
            pltpu.VMEM((1, HQ * HEAD_SIZE), jnp.bfloat16),
            pltpu.SemaphoreType.DMA((2,)),
        ],
    )(
        pltpu.with_memory_space_constraint(page_request, pltpu.MemorySpace.HBM),
        pltpu.with_memory_space_constraint(queries, pltpu.MemorySpace.HBM),
    )
    heads = lax.all_to_all(sent, ("req", "kv"), 0, 0, tiled=True)
    picked, member = kernel_call(
        select_kernel,
        (shape((256, 128), jnp.bfloat16), shape((32, 128), jnp.float32)),
        [VMEM],
        "select",
        flops=10**10,
    )(heads)
    wanted = lax.all_to_all(picked, "req", 0, 0, tiled=True)
    partial = kernel_call(
        attend_kernel,
        shape((32, MESSAGE_ROWS, 128), jnp.int16),
        [VMEM] * 6,
        "attend",
    )(
        page_request.reshape(1, -1),
        page_number.reshape(1, -1),
        lengths.reshape(1, -1),
        wanted,
        paged_key_cache,
        paged_value_cache,
    )
    partial = lax.all_to_all(partial, "req", 0, 0, tiled=True)
    merged = kernel_call(
        merge_kernel, shape((8, MESSAGE_ROWS, 128), jnp.int16), [VMEM, VMEM], "merge"
    )(partial, member)
    merged = lax.all_to_all(merged, "kv", 0, 0, tiled=True)
    return kernel_call(finish_kernel, shape((1, 4096), jnp.bfloat16), [VMEM], "finish")(merged)


def solution(mesh):
    placed = (
        P(("req", "kv"), None),
        P(("req", "kv"), None, None),
        P(("req", "kv"), None, None),
        P(("req", "kv")),
        P(("req", "kv")),
        P(),
    )
    return jax.shard_map(
        on_device, mesh=mesh, in_specs=placed, out_specs=P(("req", "kv"), None), check_vma=False
    )
```

time: 67.7 us -> 67.1 us (level)
  no operation moved by 1% of the time
where the time goes in v3:
time: 67.1 us; the launch traced here: 66.8 us
  blocking collectives  62.9 us (94%)
  Pallas kernels  3.76 us (6%)
    all_to_all x1, blocking collectives, on_device(): heads = lax.all_to_all(sent, ('req', 'kv'), 0, 0, tiled=True)  28.5 us
    all_to_all x1, blocking collectives, on_device(): partial = lax.all_to_all(partial, 'req', 0, 0, tiled=True)  13.1 us
    all_to_all x1, blocking collectives, on_device(): wanted = lax.all_to_all(picked, 'req', 0, 0, tiled=True)  11.2 us
    all_to_all x1, blocking collectives, on_device(): merged = lax.all_to_all(merged, 'kv', 0, 0, tiled=True)  10.1 us

profile of v3, /device:TPU:1, one launch (start us, length us, event | category | flops | bytes accessed | tf_op | source)
XLA Modules:
  0.0 66.8 jit_solution(6158632431686700107)
XLA Ops:
  0.0 0.8 %spread.1 = bf16[512,128]{1,0:T(8,128)(2,1)S(1)} custom-call(s32[6]{0:T(128)} %pages_in.1, bf16[1,4096]{1,0:T(2,128)(2,1)} %query_in.1), custom_call_target="tpu_custom_call" | custom-call | tf_op jit(solution)/shard_map/spread/pallas_call | solution.py:209
  0.8 28.5 %all_to_all.32 = bf16[256,2,128]{2,1,0:T(2,128)(2,1)S(1)} all-to-all(bf16[256,2,128]{2,1,0:T(2,128)(2,1)S(1)} %bitcast.7), channel_id=1, replica_groups=mesh['req'=32,'kv'=8] {'req','kv'}, dimensions={0} | all-to-all | bytes 262144 | tf_op jit(solution)/shard_map/all_to_all | solution.py:223
  29.3 0.0 copy-start
  29.3 0.0 copy-start.1
  29.3 0.0 copy-start.2
  29.3 0.0 copy-start.3
  29.3 0.0 copy-start.4
  29.3 0.4 select.1
  29.7 11.2 %all_to_all.33 = bf16[32,8,128]{2,1,0:T(8,128)(2,1)S(1)} all-to-all(bf16[32,8,128]{2,1,0:T(8,128)(2,1)S(1)} %bitcast.10), channel_id=1, replica_groups=mesh['req'=32,'kv'=8] {'req'}, dimensions={0} | all-to-all | bytes 131072 | tf_op jit(solution)/shard_map/all_to_all | solution.py:231
  40.9 0.0 copy-done
  40.9 0.0 copy-done.1
  40.9 0.0 copy-done.2
  40.9 0.0 copy-done.3
  40.9 0.0 copy-done.4
  40.9 1.0 %attend.1 = s16[32,40,128]{2,1,0:T(8,128)(2,1)S(1)} custom-call(s32[1,6]{1,0:T(1,128)S(1)} %bitcast.11, s32[1,6]{1,0:T(1,128)S(1)} %bitcast.13, s32[1,256]{1,0:T(1,128)S(1)} %bitcast.12, bf16[256,128]{1,0:T(8,128)(2,1)S(1)} %bitcast.8, bf16[6,128,1024]{2,1,0:T(8,128)(2,1)S(1)} %copy-done, bf16[6,128,1024]{2,1,0:T(8,128)(2,1)S(1)} %copy-done.1), custom_call_target="tpu_custom_call" | custom-call | tf_op jit(solution)/shard_map/attend/pallas_call | solution.py:232
  42.0 13.1 %all_to_all.34.recv = s16[32,40,128]{2,1,0:T(8,128)(2,1)S(1)} all-to-all(s16[32,40,128]{2,1,0:T(8,128)(2,1)S(1)} %attend.1), channel_id=1, replica_groups=mesh['req'=32,'kv'=8] {'req'}, dimensions={0} | all-to-all | bytes 655360 | tf_op jit(solution)/shard_map/all_to_all | solution.py:245
  55.1 0.7 %merge.1 = s16[8,40,128]{2,1,0:T(8,128)(2,1)S(1)} custom-call(s16[32,40,128]{2,1,0:T(8,128)(2,1)S(1)} %all_to_all.34.recv, f32[32,128]{1,0:T(8,128)S(1)} %get-tuple-element.8.member), custom_call_target="tpu_custom_call" | custom-call | tf_op jit(solution)/shard_map/merge/pallas_call | solution.py:246
  55.8 10.1 %all_to_all.35.recv = s16[8,40,128]{2,1,0:T(8,128)(2,1)S(1)} all-to-all(s16[8,40,128]{2,1,0:T(8,128)(2,1)S(1)} %merge.1), channel_id=1, replica_groups=mesh['req'=32,'kv'=8] {'kv'}, dimensions={0} | all-to-all | bytes 163840 | tf_op jit(solution)/shard_map/all_to_all | solution.py:249
  65.9 0.8 %finish.1 = bf16[1,4096]{1,0:T(2,128)(2,1)} custom-call(s16[8,40,128]{2,1,0:T(8,128)(2,1)S(1)} %all_to_all.35.recv), custom_call_target="tpu_custom_call" | custom-call | tf_op jit(solution)/shard_map/finish/pallas_call | solution.py:250
Async XLA Ops:
  29.3 11.6 %copy-start = (bf16[6,128,1024]{2,1,0:T(8,128)(2,1)S(1)}, bf16[6,128,1024]{2,1,0:T(8,128)(2,1)}, u32[]{:S(2)}) copy-start(bf16[6,128,1024]{2,1,0:T(8,128)(2,1)} %keys.1) | copy-start | bytes 4718596
  29.3 11.6 %copy-start.1 = (bf16[6,128,1024]{2,1,0:T(8,128)(2,1)S(1)}, bf16[6,128,1024]{2,1,0:T(8,128)(2,1)}, u32[]{:S(2)}) copy-start(bf16[6,128,1024]{2,1,0:T(8,128)(2,1)} %values.1) | copy-start | bytes 4718596
  29.3 11.6 %copy-start.2 = (s32[6]{0:T(128)S(1)}, s32[6]{0:T(128)}, u32[]{:S(2)}) copy-start(s32[6]{0:T(128)} %pages_in.1) | copy-start | bytes 76
  29.3 11.6 %copy-start.3 = (s32[256]{0:T(256)S(1)}, s32[256]{0:T(256)}, u32[]{:S(2)}) copy-start(s32[256]{0:T(256)} %param.11) | copy-start | bytes 3076
  29.3 11.6 %copy-start.4 = (s32[6]{0:T(128)S(1)}, s32[6]{0:T(128)}, u32[]{:S(2)}) copy-start(s32[6]{0:T(128)} %param.10) | copy-start | bytes 76

commit v4 on v3

--- a/solution.py
+++ b/solution.py
@@ -25,13 +25,13 @@
     first_copy.start()
     second_copy.start()
     first_copy.wait()
-    second_copy.wait()
     lane = iota((16, 128), 1)
     even = iota((16, 128), 0) % 2 == 0
     first = (lax.axis_index("req") % 16) * SLOT_ROWS
     ids = jnp.zeros((16, 128), jnp.float32)
     for s in range(SLOTS):
         ids = jnp.where(lane == first + s, pages[s].astype(jnp.float32), ids)
+    second_copy.wait()
     for h in range(HQ):
         head = query[0:1, h * 128 : (h + 1) * 128].astype(jnp.float32)
         block = jnp.where(even, jnp.broadcast_to(head, (16, 128)), ids)
@@ -144,7 +144,7 @@
     return tiles[:, 0, :] * 0.0625 + tiles[:, 1, :] * (1.0 / 524288.0), tiles[:, 2, :]
 
 
-def merge_kernel(recv, member, out):
+def merge_kernel(recv, member, out, sums_of):
     place = member[...]
     lse, power = statistics(recv)
     peak, unit, total = (jnp.zeros((32, 128), jnp.float32) for _ in range(3))
@@ -162,14 +162,15 @@
         total = jnp.where(own, sums[j], total)
     total = jnp.where(place >= 0.0, total, 1.0)
     factor = jnp.transpose(weight / total * jnp.exp2(power - unit))[0:HQ, :]
-    accs = [jnp.zeros((HQ, 128), jnp.float32) for _ in range(8)]
+    sums_of[...] = jnp.zeros(sums_of.shape, jnp.float32)
     for g in range(32):
         row = recv[g, 0:HQ, :].astype(jnp.int32).astype(jnp.float32)
         row = row * jnp.broadcast_to(factor[:, g : g + 1], (HQ, 128))
-        at = jnp.broadcast_to(place[g : g + 1, :], (HQ, 128))
-        accs = [acc + jnp.where(at == j, row, 0.0) for j, acc in enumerate(accs)]
+        j = jnp.max(place[g : g + 1, 0:1]).astype(jnp.int32)
+        j = jnp.where(j < 0, 8, j)
+        sums_of[j + 9 * (g % 2)] = sums_of[j + 9 * (g % 2)] + row
     for j in range(8):
-        out[j, 0:HQ, :] = jnp.round(accs[j]).astype(jnp.int32).astype(jnp.int16)
+        out[j, 0:HQ, :] = jnp.round(sums_of[j] + sums_of[j + 9]).astype(jnp.int32).astype(jnp.int16)
         lse = jnp.where(sums[j] > 0.0, tops[j] + jnp.log(jnp.maximum(sums[j], 1e-30)), ABSENT)
         out[j, HQ:MESSAGE_ROWS, :] = statistics_tile(lse, units[j])
 
@@ -244,7 +245,11 @@
     )
     partial = lax.all_to_all(partial, "req", 0, 0, tiled=True)
     merged = kernel_call(
-        merge_kernel, shape((8, MESSAGE_ROWS, 128), jnp.int16), [VMEM, VMEM], "merge"
+        merge_kernel,
+        shape((8, MESSAGE_ROWS, 128), jnp.int16),
+        [VMEM, VMEM],
+        "merge",
+        [pltpu.VMEM((18, HQ, 128), jnp.float32)],
     )(partial, member)
     merged = lax.all_to_all(merged, "kv", 0, 0, tiled=True)
     return kernel_call(finish_kernel, shape((1, 4096), jnp.bfloat16), [VMEM], "finish")(merged)

time: 67.1 us -> 66.8 us (level)
  no operation moved by 1% of the time
where the time goes in v4:
time: 66.8 us; the launch traced here: 66.5 us
  blocking collectives  62.9 us (94%)
  Pallas kernels  3.53 us (5%)
    all_to_all x1, blocking collectives, on_device(): heads = lax.all_to_all(sent, ('req', 'kv'), 0, 0, tiled=True)  28.5 us
    all_to_all x1, blocking collectives, on_device(): partial = lax.all_to_all(partial, 'req', 0, 0, tiled=True)  13.1 us
    all_to_all x1, blocking collectives, on_device(): wanted = lax.all_to_all(picked, 'req', 0, 0, tiled=True)  11.2 us
    all_to_all x1, blocking collectives, on_device(): merged = lax.all_to_all(merged, 'kv', 0, 0, tiled=True)  10.1 us

profile of v4, /device:TPU:1, one launch (start us, length us, event | category | flops | bytes accessed | tf_op | source)
XLA Modules:
  0.0 66.5 jit_solution(16164055879557836402)
XLA Ops:
  0.0 0.8 %spread.1 = bf16[512,128]{1,0:T(8,128)(2,1)S(1)} custom-call(s32[6]{0:T(128)} %pages_in.1, bf16[1,4096]{1,0:T(2,128)(2,1)} %query_in.1), custom_call_target="tpu_custom_call" | custom-call | tf_op jit(solution)/shard_map/spread/pallas_call | solution.py:210
  0.8 28.5 %all_to_all.32 = bf16[256,2,128]{2,1,0:T(2,128)(2,1)S(1)} all-to-all(bf16[256,2,128]{2,1,0:T(2,128)(2,1)S(1)} %bitcast.7), channel_id=1, replica_groups=mesh['req'=32,'kv'=8] {'req','kv'}, dimensions={0} | all-to-all | bytes 262144 | tf_op jit(solution)/shard_map/all_to_all | solution.py:224
  29.3 0.0 copy-start
  29.3 0.0 copy-start.1
  29.3 0.0 copy-start.2
  29.3 0.0 copy-start.3
  29.3 0.0 copy-start.4
  29.3 0.4 select.1
  29.7 11.2 %all_to_all.33 = bf16[32,8,128]{2,1,0:T(8,128)(2,1)S(1)} all-to-all(bf16[32,8,128]{2,1,0:T(8,128)(2,1)S(1)} %bitcast.10), channel_id=1, replica_groups=mesh['req'=32,'kv'=8] {'req'}, dimensions={0} | all-to-all | bytes 131072 | tf_op jit(solution)/shard_map/all_to_all | solution.py:232
  40.9 0.0 copy-done
  40.9 0.0 copy-done.1
  40.9 0.0 copy-done.2
  40.9 0.0 copy-done.3
  40.9 0.0 copy-done.4
  40.9 1.0 %attend.1 = s16[32,40,128]{2,1,0:T(8,128)(2,1)S(1)} custom-call(s32[1,6]{1,0:T(1,128)S(1)} %bitcast.11, s32[1,6]{1,0:T(1,128)S(1)} %bitcast.13, s32[1,256]{1,0:T(1,128)S(1)} %bitcast.12, bf16[256,128]{1,0:T(8,128)(2,1)S(1)} %bitcast.8, bf16[6,128,1024]{2,1,0:T(8,128)(2,1)S(1)} %copy-done, bf16[6,128,1024]{2,1,0:T(8,128)(2,1)S(1)} %copy-done.1), custom_call_target="tpu_custom_call" | custom-call | tf_op jit(solution)/shard_map/attend/pallas_call | solution.py:233
  41.9 13.1 %all_to_all.34.recv = s16[32,40,128]{2,1,0:T(8,128)(2,1)S(1)} all-to-all(s16[32,40,128]{2,1,0:T(8,128)(2,1)S(1)} %attend.1), channel_id=1, replica_groups=mesh['req'=32,'kv'=8] {'req'}, dimensions={0} | all-to-all | bytes 655360 | tf_op jit(solution)/shard_map/all_to_all | solution.py:246
  55.1 0.5 merge.1
  55.6 10.1 %all_to_all.35.recv = s16[8,40,128]{2,1,0:T(8,128)(2,1)S(1)} all-to-all(s16[8,40,128]{2,1,0:T(8,128)(2,1)S(1)} %merge.1), channel_id=1, replica_groups=mesh['req'=32,'kv'=8] {'kv'}, dimensions={0} | all-to-all | bytes 163840 | tf_op jit(solution)/shard_map/all_to_all | solution.py:254
  65.7 0.8 %finish.1 = bf16[1,4096]{1,0:T(2,128)(2,1)} custom-call(s16[8,40,128]{2,1,0:T(8,128)(2,1)S(1)} %all_to_all.35.recv), custom_call_target="tpu_custom_call" | custom-call | tf_op jit(solution)/shard_map/finish/pallas_call | solution.py:255
Async XLA Ops:
  29.3 11.6 %copy-start = (bf16[6,128,1024]{2,1,0:T(8,128)(2,1)S(1)}, bf16[6,128,1024]{2,1,0:T(8,128)(2,1)}, u32[]{:S(2)}) copy-start(bf16[6,128,1024]{2,1,0:T(8,128)(2,1)} %keys.1) | copy-start | bytes 4718596
  29.3 11.6 %copy-start.1 = (bf16[6,128,1024]{2,1,0:T(8,128)(2,1)S(1)}, bf16[6,128,1024]{2,1,0:T(8,128)(2,1)}, u32[]{:S(2)}) copy-start(bf16[6,128,1024]{2,1,0:T(8,128)(2,1)} %values.1) | copy-start | bytes 4718596
  29.3 11.6 %copy-start.2 = (s32[6]{0:T(128)S(1)}, s32[6]{0:T(128)}, u32[]{:S(2)}) copy-start(s32[6]{0:T(128)} %pages_in.1) | copy-start | bytes 76
  29.3 11.6 %copy-start.3 = (s32[256]{0:T(256)S(1)}, s32[256]{0:T(256)}, u32[]{:S(2)}) copy-start(s32[256]{0:T(256)} %param.11) | copy-start | bytes 3076
  29.3 11.6 %copy-start.4 = (s32[6]{0:T(128)S(1)}, s32[6]{0:T(128)}, u32[]{:S(2)}) copy-start(s32[6]{0:T(128)} %param.10) | copy-start | bytes 76

commit v5 on v4

--- a/solution.py
+++ b/solution.py
@@ -11,6 +11,7 @@
 SLOTS = 6
 SLOT_ROWS = 8
 MESSAGE_ROWS = 40
+SHORT_ROWS = 34
 ABSENT = -2048.0
 TOP = 32767.0
 
@@ -81,16 +82,19 @@
     slot, head = r // 64 * 2 + r // 8 % 2, r // 16 % 4 * 8 + r % 8
     order = (c == head * SLOT_ROWS + slot).astype(jnp.float32).astype(jnp.bfloat16)
     query = jnp.dot(order, recv[...], preferred_element_type=jnp.float32)
-    upper = iota((rows, 128), 0) % 8 < 4
-    both = jnp.concatenate([jnp.where(upper, query, 0.0), jnp.where(upper, 0.0, query)], axis=1)
-    both = both.astype(jnp.bfloat16)
+    upper = iota((64, 128), 0) % 8 < 4
+    first = iota((64, 128), 0) % 16 < 8
     lane = iota((8, 128), 1).astype(jnp.float32)
-    scores = []
-    for p in range(SLOTS // 2):
+    lanes = iota((64, 128), 1)
+
+    def score(p):
+        rows = query[64 * p : 64 * p + 64, :]
+        both = jnp.concatenate([jnp.where(upper, rows, 0.0), jnp.where(upper, 0.0, rows)], axis=1)
+        both = both.astype(jnp.bfloat16)
+        scores = []
         for i in range(4):
-            at = 64 * p + 16 * i
             tile = lax.dot_general(
-                both[at : at + 16, :],
+                both[16 * i : 16 * i + 16, :],
                 keys[2 * p : 2 * p + 2, :, 256 * i : 256 * i + 256].reshape(256, 256),
                 (((1,), (1,)), ((), ())),
                 preferred_element_type=jnp.float32,
@@ -98,37 +102,62 @@
             for n in range(2):
                 part = tile[8 * n : 8 * n + 8, 128 * n : 128 * n + 128] * HEAD_SIZE**-0.5
                 scores.append(jnp.where(lane < limits[2 * p + n], part, -1e30))
-    scores = jnp.concatenate(scores, axis=0)
-    top = jnp.max(scores, axis=1, keepdims=True)
-    weights = jnp.exp(scores - top)
-    total = jnp.sum(weights, axis=1, keepdims=True)
-    first = iota((rows, 128), 0) % 16 < 8
-    wide = jnp.concatenate([jnp.where(first, weights, 0.0), jnp.where(first, 0.0, weights)], axis=1)
-    wide = wide.astype(jnp.bfloat16)
-    outs = []
-    for p in range(SLOTS // 2):
+        return jnp.concatenate(scores, axis=0)
+
+    def weigh(scores):
+        top = jnp.max(scores, axis=1, keepdims=True)
+        weights = jnp.exp(scores - top)
+        total = jnp.sum(weights, axis=1, keepdims=True)
+        wide = [jnp.where(first, weights, 0.0), jnp.where(first, 0.0, weights)]
+        return jnp.concatenate(wide, axis=1).astype(jnp.bfloat16), top, total
+
+    def add_up(p, wide):
+        outs = []
         for i in range(4):
-            at = 64 * p + 16 * i
             tile = jnp.dot(
-                wide[at : at + 16, :],
+                wide[16 * i : 16 * i + 16, :],
                 values[2 * p : 2 * p + 2, :, 256 * i : 256 * i + 256].reshape(256, 256),
                 preferred_element_type=jnp.float32,
             )
             outs.append(jnp.where(upper[0:16, :], tile[:, :128], tile[:, 128:]))
-    outs = jnp.concatenate(outs, axis=0) / total
-    largest = jnp.max(jnp.abs(outs), axis=1, keepdims=True)
-    power = jnp.ceil(jnp.log2(jnp.maximum(largest, 1e-30)))
-    whole = jnp.round(outs * (jnp.exp2(-power) * TOP)).astype(jnp.int32).astype(jnp.int16)
-    lanes = iota((rows, 128), 1)
-    stats = jnp.where(lanes == 0, top + jnp.log(total), jnp.where(lanes == 1, power, 0.0))
+        return jnp.concatenate(outs, axis=0)
+
+    def send(p, outs, top, total):
+        outs = outs / total
+        largest = jnp.max(jnp.abs(outs), axis=1, keepdims=True)
+        power = jnp.ceil(jnp.log2(jnp.maximum(largest, 1e-30)))
+        whole = jnp.round(outs * (jnp.exp2(-power) * TOP))
+        stats = jnp.where(lanes == 0, top + jnp.log(total), jnp.where(lanes == 1, power, 0.0))
+        for n in range(2):
+            target = targets[2 * p + n]
+            starts = [16 * i + 8 * n for i in range(4)]
+            turned = jnp.transpose(jnp.concatenate([stats[a : a + 8, :] for a in starts], axis=0))
+            line = statistics_row(turned[0:1, :], turned[1:2, :])
+            block = jnp.concatenate([whole[a : a + 8, :] for a in starts] + [line], axis=0)
+            past = target * SHORT_ROWS % 8
+            block = pltpu.roll(block, past, 0).astype(jnp.int32)
+            at = pl.ds(pl.multiple_of(target * SHORT_ROWS - past, 8), MESSAGE_ROWS)
+            out[at, :] = (out[at, :].astype(jnp.int32) + block).astype(jnp.int16)
+
     out[...] = jnp.zeros(out.shape, jnp.int16)
-    for s in range(SLOTS):
-        target = targets[s]
-        starts = [64 * (s // 2) + 16 * i + 8 * (s % 2) for i in range(4)]
-        out[target, 0:HQ, :] = jnp.concatenate([whole[a : a + 8, :] for a in starts], axis=0)
-        turned = jnp.transpose(jnp.concatenate([stats[a : a + 8, :] for a in starts], axis=0))
-        turned = jnp.concatenate([turned[0:8, :], jnp.zeros((8, 96), jnp.float32)], axis=1)
-        out[target, HQ:MESSAGE_ROWS, :] = statistics_tile(turned[0:1, :], turned[1:2, :])
+    scores = [score(0), score(1)]
+    soft = [weigh(scores[0])]
+    scores.append(score(2))
+    sums = [add_up(0, soft[0][0])]
+    soft.append(weigh(scores[1]))
+    sums.append(add_up(1, soft[1][0]))
+    soft.append(weigh(scores[2]))
+    send(0, sums[0], *soft[0][1:])
+    sums.append(add_up(2, soft[2][0]))
+    send(1, sums[1], *soft[1][1:])
+    send(2, sums[2], *soft[2][1:])
+
+
+def statistics_row(lse, power):
+    coarse = jnp.round(lse * 16.0)
+    fine = jnp.round((lse - coarse * 0.0625) * 524288.0)
+    line = jnp.concatenate([coarse, fine, power, jnp.zeros((1, 32), jnp.float32)], axis=1)
+    return jnp.where(iota((8, 128), 0) == 0, jnp.broadcast_to(line, (8, 128)), 0.0)
 
 
 def statistics_tile(lse, power):
@@ -146,7 +175,13 @@
 
 def merge_kernel(recv, member, out, sums_of):
     place = member[...]
-    lse, power = statistics(recv)
+    lines = [
+        recv[SHORT_ROWS * g + HQ : SHORT_ROWS * (g + 1), :].astype(jnp.int32).astype(jnp.float32)[0:1]
+        for g in range(32)
+    ]
+    tile = jnp.concatenate(lines, axis=0)
+    lse = tile * 0.0625 + pltpu.roll(tile, 96, 1) * (1.0 / 524288.0)
+    power = pltpu.roll(tile, 64, 1)
     peak, unit, total = (jnp.zeros((32, 128), jnp.float32) for _ in range(3))
     tops, units, sums = [], [], []
     for j in range(8):
@@ -164,7 +199,7 @@
     factor = jnp.transpose(weight / total * jnp.exp2(power - unit))[0:HQ, :]
     sums_of[...] = jnp.zeros(sums_of.shape, jnp.float32)
     for g in range(32):
-        row = recv[g, 0:HQ, :].astype(jnp.int32).astype(jnp.float32)
+        row = recv[SHORT_ROWS * g : SHORT_ROWS * g + HQ, :].astype(jnp.int32).astype(jnp.float32)
         row = row * jnp.broadcast_to(factor[:, g : g + 1], (HQ, 128))
         j = jnp.max(place[g : g + 1, 0:1]).astype(jnp.int32)
         j = jnp.where(j < 0, 8, j)
@@ -232,7 +267,7 @@
     wanted = lax.all_to_all(picked, "req", 0, 0, tiled=True)
     partial = kernel_call(
         attend_kernel,
-        shape((32, MESSAGE_ROWS, 128), jnp.int16),
+        shape((32 * SHORT_ROWS, 128), jnp.int16),
         [VMEM] * 6,
         "attend",
     )(
@@ -243,7 +278,8 @@
         paged_key_cache,
         paged_value_cache,
     )
-    partial = lax.all_to_all(partial, "req", 0, 0, tiled=True)
+    partial = partial.reshape(32, SHORT_ROWS // 2, 2, 128)
+    partial = lax.all_to_all(partial, "req", 0, 0, tiled=True).reshape(32 * SHORT_ROWS, 128)
     merged = kernel_call(
         merge_kernel,
         shape((8, MESSAGE_ROWS, 128), jnp.int16),

time: 66.8 us -> 66.4 us (level)
  no operation moved by 1% of the time
where the time goes in v5:
time: 66.4 us; the launch traced here: 66.2 us
  blocking collectives  62.3 us (94%)
  Pallas kernels  3.77 us (6%)
    all_to_all x1, blocking collectives, on_device(): heads = lax.all_to_all(sent, ('req', 'kv'), 0, 0, tiled=True)  28.5 us
    all_to_all x1, blocking collectives, on_device(): lax.all_to_all(partial, 'req', 0, 0, tiled=True)  12.7 us
    all_to_all x1, blocking collectives, on_device(): wanted = lax.all_to_all(picked, 'req', 0, 0, tiled=True)  11.2 us
    all_to_all x1, blocking collectives, on_device(): merged = lax.all_to_all(merged, 'kv', 0, 0, tiled=True)  9.96 us

profile of v5, /device:TPU:1, one launch (start us, length us, event | category | flops | bytes accessed | tf_op | source)
XLA Modules:
  0.0 66.2 jit_solution(9373896764291176023)
XLA Ops:
  0.0 0.8 %spread.1 = bf16[512,128]{1,0:T(8,128)(2,1)S(1)} custom-call(s32[6]{0:T(128)} %pages_in.1, bf16[1,4096]{1,0:T(2,128)(2,1)} %query_in.1), custom_call_target="tpu_custom_call" | custom-call | tf_op jit(solution)/shard_map/spread/pallas_call | solution.py:245
  0.8 28.5 %all_to_all.32 = bf16[256,2,128]{2,1,0:T(2,128)(2,1)S(1)} all-to-all(bf16[256,2,128]{2,1,0:T(2,128)(2,1)S(1)} %bitcast.11), channel_id=1, replica_groups=mesh['req'=32,'kv'=8] {'req','kv'}, dimensions={0} | all-to-all | bytes 262144 | tf_op jit(solution)/shard_map/all_to_all | solution.py:259
  29.3 0.0 copy-start
  29.3 0.0 copy-start.1
  29.3 0.0 copy-start.2
  29.3 0.0 copy-start.3
  29.3 0.0 copy-start.4
  29.3 0.4 select.1
  29.7 11.2 %all_to_all.33 = bf16[32,8,128]{2,1,0:T(8,128)(2,1)S(1)} all-to-all(bf16[32,8,128]{2,1,0:T(8,128)(2,1)S(1)} %bitcast.14), channel_id=1, replica_groups=mesh['req'=32,'kv'=8] {'req'}, dimensions={0} | all-to-all | bytes 131072 | tf_op jit(solution)/shard_map/all_to_all | solution.py:267
  40.9 0.0 copy-done
  40.9 0.0 copy-done.1
  40.9 0.0 copy-done.2
  40.9 0.0 copy-done.3
  40.9 0.0 copy-done.4
  40.9 1.2 %attend.1 = s16[1088,128]{1,0:T(8,128)(2,1)S(1)} custom-call(s32[1,6]{1,0:T(1,128)S(1)} %bitcast.15, s32[1,6]{1,0:T(1,128)S(1)} %bitcast.17, s32[1,256]{1,0:T(1,128)S(1)} %bitcast.16, bf16[256,128]{1,0:T(8,128)(2,1)S(1)} %bitcast.12, bf16[6,128,1024]{2,1,0:T(8,128)(2,1)S(1)} %copy-done, bf16[6,128,1024]{2,1,0:T(8,128)(2,1)S(1)} %copy-done.1), custom_call_target="tpu_custom_call" | custom-call | tf_op jit(solution)/shard_map/attend/pallas_call | solution.py:268
  42.1 12.7 %all_to_all.34 = s16[32,17,2,128]{3,2,1,0:T(2,128)(2,1)S(1)} all-to-all(s16[32,17,2,128]{3,2,1,0:T(2,128)(2,1)S(1)} %bitcast.9), channel_id=1, replica_groups=mesh['req'=32,'kv'=8] {'req'}, dimensions={0} | all-to-all | bytes 557056 | tf_op jit(solution)/shard_map/all_to_all | solution.py:282
  54.8 0.5 merge.1
  55.3 10.0 %all_to_all.35.recv = s16[8,40,128]{2,1,0:T(8,128)(2,1)S(1)} all-to-all(s16[8,40,128]{2,1,0:T(8,128)(2,1)S(1)} %merge.1), channel_id=1, replica_groups=mesh['req'=32,'kv'=8] {'kv'}, dimensions={0} | all-to-all | bytes 163840 | tf_op jit(solution)/shard_map/all_to_all | solution.py:290
  65.3 0.8 %finish.1 = bf16[1,4096]{1,0:T(2,128)(2,1)} custom-call(s16[8,40,128]{2,1,0:T(8,128)(2,1)S(1)} %all_to_all.35.recv), custom_call_target="tpu_custom_call" | custom-call | tf_op jit(solution)/shard_map/finish/pallas_call | solution.py:291
Async XLA Ops:
  29.3 11.6 %copy-start = (bf16[6,128,1024]{2,1,0:T(8,128)(2,1)S(1)}, bf16[6,128,1024]{2,1,0:T(8,128)(2,1)}, u32[]{:S(2)}) copy-start(bf16[6,128,1024]{2,1,0:T(8,128)(2,1)} %keys.1) | copy-start | bytes 4718596
  29.3 11.6 %copy-start.1 = (bf16[6,128,1024]{2,1,0:T(8,128)(2,1)S(1)}, bf16[6,128,1024]{2,1,0:T(8,128)(2,1)}, u32[]{:S(2)}) copy-start(bf16[6,128,1024]{2,1,0:T(8,128)(2,1)} %values.1) | copy-start | bytes 4718596
  29.3 11.6 %copy-start.2 = (s32[6]{0:T(128)S(1)}, s32[6]{0:T(128)}, u32[]{:S(2)}) copy-start(s32[6]{0:T(128)} %pages_in.1) | copy-start | bytes 76
  29.3 11.6 %copy-start.3 = (s32[256]{0:T(256)S(1)}, s32[256]{0:T(256)}, u32[]{:S(2)}) copy-start(s32[256]{0:T(256)} %param.11) | copy-start | bytes 3076
  29.3 11.6 %copy-start.4 = (s32[6]{0:T(128)S(1)}, s32[6]{0:T(128)}, u32[]{:S(2)}) copy-start(s32[6]{0:T(128)} %param.10) | copy-start | bytes 76

commit v6 on v5

--- a/solution.py
+++ b/solution.py
@@ -126,18 +126,24 @@
         outs = outs / total
         largest = jnp.max(jnp.abs(outs), axis=1, keepdims=True)
         power = jnp.ceil(jnp.log2(jnp.maximum(largest, 1e-30)))
-        whole = jnp.round(outs * (jnp.exp2(-power) * TOP))
-        stats = jnp.where(lanes == 0, top + jnp.log(total), jnp.where(lanes == 1, power, 0.0))
+        whole = jnp.round(outs * (jnp.exp2(-power) * TOP)).astype(jnp.int32).astype(jnp.int16)
+        lse = top + jnp.log(total)
+        coarse = jnp.round(lse * 16.0)
+        fine = jnp.round((lse - coarse * 0.0625) * 524288.0)
+        columns = []
+        for kind in (coarse, fine, power):
+            for i in range(0, 64, 16):
+                pair = [jnp.broadcast_to(kind[i + n : i + n + 8, :], (8, 128)) for n in (0, 8)]
+                columns.append(jnp.where(lanes[0:8] == 0, *pair))
+        columns.append(jnp.zeros((32, 128), jnp.float32))
+        lines = jnp.transpose(jnp.concatenate(columns, axis=0))[0:8, :]
+        lines = lines.astype(jnp.int32).astype(jnp.int16)
         for n in range(2):
             target = targets[2 * p + n]
-            starts = [16 * i + 8 * n for i in range(4)]
-            turned = jnp.transpose(jnp.concatenate([stats[a : a + 8, :] for a in starts], axis=0))
-            line = statistics_row(turned[0:1, :], turned[1:2, :])
-            block = jnp.concatenate([whole[a : a + 8, :] for a in starts] + [line], axis=0)
-            past = target * SHORT_ROWS % 8
-            block = pltpu.roll(block, past, 0).astype(jnp.int32)
-            at = pl.ds(pl.multiple_of(target * SHORT_ROWS - past, 8), MESSAGE_ROWS)
-            out[at, :] = (out[at, :].astype(jnp.int32) + block).astype(jnp.int16)
+            block = jnp.concatenate([whole[i + 8 * n : i + 8 * n + 8] for i in range(0, 64, 16)], axis=0)
+            for i in range(HQ // 2):
+                out[target, i, :, :] = block[2 * i : 2 * i + 2, :]
+            out[target, HQ // 2, :, :] = lines[n : n + 2, :]
 
     out[...] = jnp.zeros(out.shape, jnp.int16)
     scores = [score(0), score(1)]
@@ -151,13 +157,6 @@
     sums.append(add_up(2, soft[2][0]))
     send(1, sums[1], *soft[1][1:])
     send(2, sums[2], *soft[2][1:])
-
-
-def statistics_row(lse, power):
-    coarse = jnp.round(lse * 16.0)
-    fine = jnp.round((lse - coarse * 0.0625) * 524288.0)
-    line = jnp.concatenate([coarse, fine, power, jnp.zeros((1, 32), jnp.float32)], axis=1)
-    return jnp.where(iota((8, 128), 0) == 0, jnp.broadcast_to(line, (8, 128)), 0.0)
 
 
 def statistics_tile(lse, power):
@@ -267,7 +266,7 @@
     wanted = lax.all_to_all(picked, "req", 0, 0, tiled=True)
     partial = kernel_call(
         attend_kernel,
-        shape((32 * SHORT_ROWS, 128), jnp.int16),
+        shape((32, SHORT_ROWS // 2, 2, 128), jnp.int16),
         [VMEM] * 6,
         "attend",
     )(
@@ -278,7 +277,6 @@
         paged_key_cache,
         paged_value_cache,
     )
-    partial = partial.reshape(32, SHORT_ROWS // 2, 2, 128)
     partial = lax.all_to_all(partial, "req", 0, 0, tiled=True).reshape(32 * SHORT_ROWS, 128)
     merged = kernel_call(
         merge_kernel,

time: 66.4 us -> 66.3 us (level)
  no operation moved by 1% of the time
where the time goes in v6:
time: 66.3 us; the launch traced here: 66 us
  blocking collectives  62.3 us (94%)
  Pallas kernels  3.62 us (5%)
    all_to_all x1, blocking collectives, on_device(): heads = lax.all_to_all(sent, ('req', 'kv'), 0, 0, tiled=True)  28.5 us
    all_to_all x1, blocking collectives, on_device(): lax.all_to_all(partial, 'req', 0, 0, tiled=True)  12.7 us
    all_to_all x1, blocking collectives, on_device(): wanted = lax.all_to_all(picked, 'req', 0, 0, tiled=True)  11.2 us
    all_to_all x1, blocking collectives, on_device(): merged = lax.all_to_all(merged, 'kv', 0, 0, tiled=True)  9.96 us

profile of v6, /device:TPU:1, one launch (start us, length us, event | category | flops | bytes accessed | tf_op | source)
XLA Modules:
  0.0 66.0 jit_solution(15977864982087656172)
XLA Ops:
  0.0 0.8 %spread.1 = bf16[512,128]{1,0:T(8,128)(2,1)S(1)} custom-call(s32[6]{0:T(128)} %pages_in.1, bf16[1,4096]{1,0:T(2,128)(2,1)} %query_in.1), custom_call_target="tpu_custom_call" | custom-call | tf_op jit(solution)/shard_map/spread/pallas_call | solution.py:244
  0.8 28.5 %all_to_all.32 = bf16[256,2,128]{2,1,0:T(2,128)(2,1)S(1)} all-to-all(bf16[256,2,128]{2,1,0:T(2,128)(2,1)S(1)} %bitcast.9), channel_id=1, replica_groups=mesh['req'=32,'kv'=8] {'req','kv'}, dimensions={0} | all-to-all | bytes 262144 | tf_op jit(solution)/shard_map/all_to_all | solution.py:258
  29.3 0.0 copy-start
  29.3 0.0 copy-start.1
  29.3 0.0 copy-start.2
  29.3 0.0 copy-start.3
  29.3 0.0 copy-start.4
  29.3 0.4 select.1
  29.7 11.2 %all_to_all.33 = bf16[32,8,128]{2,1,0:T(8,128)(2,1)S(1)} all-to-all(bf16[32,8,128]{2,1,0:T(8,128)(2,1)S(1)} %bitcast.12), channel_id=1, replica_groups=mesh['req'=32,'kv'=8] {'req'}, dimensions={0} | all-to-all | bytes 131072 | tf_op jit(solution)/shard_map/all_to_all | solution.py:266
  40.9 0.0 copy-done
  40.9 0.0 copy-done.1
  40.9 0.0 copy-done.2
  40.9 0.0 copy-done.3
  40.9 0.0 copy-done.4
  40.9 1.1 %attend.1 = s16[32,17,2,128]{3,2,1,0:T(2,128)(2,1)S(1)} custom-call(s32[1,6]{1,0:T(1,128)S(1)} %bitcast.13, s32[1,6]{1,0:T(1,128)S(1)} %bitcast.15, s32[1,256]{1,0:T(1,128)S(1)} %bitcast.14, bf16[256,128]{1,0:T(8,128)(2,1)S(1)} %bitcast.10, bf16[6,128,1024]{2,1,0:T(8,128)(2,1)S(1)} %copy-done, bf16[6,128,1024]{2,1,0:T(8,128)(2,1)S(1)} %copy-done.1), custom_call_target="tpu_custom_call" | custom-call | tf_op jit(solution)/shard_map/attend/pallas_call | solution.py:267
  42.0 12.7 %all_to_all.34 = s16[32,17,2,128]{3,2,1,0:T(2,128)(2,1)S(1)} all-to-all(s16[32,17,2,128]{3,2,1,0:T(2,128)(2,1)S(1)} %attend.1), channel_id=1, replica_groups=mesh['req'=32,'kv'=8] {'req'}, dimensions={0} | all-to-all | bytes 557056 | tf_op jit(solution)/shard_map/all_to_all | solution.py:280
  54.6 0.5 merge.1
  55.2 10.0 %all_to_all.35.recv = s16[8,40,128]{2,1,0:T(8,128)(2,1)S(1)} all-to-all(s16[8,40,128]{2,1,0:T(8,128)(2,1)S(1)} %merge.1), channel_id=1, replica_groups=mesh['req'=32,'kv'=8] {'kv'}, dimensions={0} | all-to-all | bytes 163840 | tf_op jit(solution)/shard_map/all_to_all | solution.py:288
  65.2 0.8 %finish.1 = bf16[1,4096]{1,0:T(2,128)(2,1)} custom-call(s16[8,40,128]{2,1,0:T(8,128)(2,1)S(1)} %all_to_all.35.recv), custom_call_target="tpu_custom_call" | custom-call | tf_op jit(solution)/shard_map/finish/pallas_call | solution.py:289
Async XLA Ops:
  29.3 11.6 %copy-start = (bf16[6,128,1024]{2,1,0:T(8,128)(2,1)S(1)}, bf16[6,128,1024]{2,1,0:T(8,128)(2,1)}, u32[]{:S(2)}) copy-start(bf16[6,128,1024]{2,1,0:T(8,128)(2,1)} %keys.1) | copy-start | bytes 4718596
  29.3 11.6 %copy-start.1 = (bf16[6,128,1024]{2,1,0:T(8,128)(2,1)S(1)}, bf16[6,128,1024]{2,1,0:T(8,128)(2,1)}, u32[]{:S(2)}) copy-start(bf16[6,128,1024]{2,1,0:T(8,128)(2,1)} %values.1) | copy-start | bytes 4718596
  29.3 11.6 %copy-start.2 = (s32[6]{0:T(128)S(1)}, s32[6]{0:T(128)}, u32[]{:S(2)}) copy-start(s32[6]{0:T(128)} %pages_in.1) | copy-start | bytes 76
  29.3 11.6 %copy-start.3 = (s32[256]{0:T(256)S(1)}, s32[256]{0:T(256)}, u32[]{:S(2)}) copy-start(s32[256]{0:T(256)} %param.11) | copy-start | bytes 3076
  29.3 11.6 %copy-start.4 = (s32[6]{0:T(128)S(1)}, s32[6]{0:T(128)}, u32[]{:S(2)}) copy-start(s32[6]{0:T(128)} %param.10) | copy-start | bytes 76

commit v7 on v6

--- a/solution.py
+++ b/solution.py
@@ -9,7 +9,6 @@
 HEAD_SIZE = 128
 PAGE = 128
 SLOTS = 6
-SLOT_ROWS = 8
 MESSAGE_ROWS = 40
 SHORT_ROWS = 34
 ABSENT = -2048.0
@@ -28,7 +27,7 @@
     first_copy.wait()
     lane = iota((16, 128), 1)
     even = iota((16, 128), 0) % 2 == 0
-    first = (lax.axis_index("req") % 16) * SLOT_ROWS
+    first = (lax.axis_index("req") % 16) * SLOTS
     ids = jnp.zeros((16, 128), jnp.float32)
     for s in range(SLOTS):
         ids = jnp.where(lane == first + s, pages[s].astype(jnp.float32), ids)
@@ -56,12 +55,12 @@
         got = lax.dot_general(
             hot, rows, (((0,), (0,)), ((), ())), preferred_element_type=jnp.float32
         )
-        out[128 * n : 128 * n + 128, :] = got.astype(jnp.bfloat16)
-        mine = (wanted // 8 == group) & (lane % 8 < SLOTS)
+        out[16 * SLOTS * n : 16 * SLOTS * (n + 1), :] = got[0 : 16 * SLOTS].astype(jnp.bfloat16)
+        mine = (wanted // 8 == group) & (lane < 16 * SLOTS)
         spots.append(jnp.where(mine, wanted % 8 + 1, 0).astype(jnp.float32))
     dev, lanes = iota((32, 128), 0), iota((32, 128), 1)
     both = jnp.where(dev < 16, spots[0], spots[1])
-    own = jnp.where(lanes // 8 == dev % 16, both, 0.0)
+    own = jnp.where(lanes // SLOTS == dev % 16, both, 0.0)
     place = jnp.sum(own, axis=1, keepdims=True) - 1.0
     member[...] = jnp.broadcast_to(place, (32, 128))
 
@@ -78,9 +77,9 @@
         group = jnp.max(whose[:, s : s + 1].astype(jnp.float32)).astype(jnp.int32)
         targets.append(lax.shift_right_logical(group, 3))
     rows = SLOTS * HQ
-    r, c = iota((rows, 256), 0), iota((rows, 256), 1)
+    r, c = iota((rows, rows), 0), iota((rows, rows), 1)
     slot, head = r // 64 * 2 + r // 8 % 2, r // 16 % 4 * 8 + r % 8
-    order = (c == head * SLOT_ROWS + slot).astype(jnp.float32).astype(jnp.bfloat16)
+    order = (c == head * SLOTS + slot).astype(jnp.float32).astype(jnp.bfloat16)
     query = jnp.dot(order, recv[...], preferred_element_type=jnp.float32)
     upper = iota((64, 128), 0) % 8 < 4
     first = iota((64, 128), 0) % 16 < 8
@@ -258,12 +257,13 @@
     heads = lax.all_to_all(sent, ("req", "kv"), 0, 0, tiled=True)
     picked, member = kernel_call(
         select_kernel,
-        (shape((256, 128), jnp.bfloat16), shape((32, 128), jnp.float32)),
+        (shape((HQ * SLOTS, 128), jnp.bfloat16), shape((32, 128), jnp.float32)),
         [VMEM],
         "select",
         flops=10**10,
     )(heads)
-    wanted = lax.all_to_all(picked, "req", 0, 0, tiled=True)
+    picked = picked.reshape(HQ, SLOTS // 2, 2, 128)
+    wanted = lax.all_to_all(picked, "req", 0, 0, tiled=True).reshape(HQ * SLOTS, 128)
     partial = kernel_call(
         attend_kernel,
         shape((32, SHORT_ROWS // 2, 2, 128), jnp.int16),

time: 66.3 us -> 66.2 us (level)
  no operation moved by 1% of the time
where the time goes in v7:
time: 66.2 us; the launch traced here: 65.9 us
  blocking collectives  62.2 us (94%)
  Pallas kernels  3.59 us (5%)
    all_to_all x1, blocking collectives, on_device(): heads = lax.all_to_all(sent, ('req', 'kv'), 0, 0, tiled=True)  28.5 us
    all_to_all x1, blocking collectives, on_device(): lax.all_to_all(partial, 'req', 0, 0, tiled=True)  12.6 us
    all_to_all x1, blocking collectives, on_device(): lax.all_to_all(picked, 'req', 0, 0, tiled=True).reshape(HQ * SLOTS, 128)  11.1 us
    all_to_all x1, blocking collectives, on_device(): merged = lax.all_to_all(merged, 'kv', 0, 0, tiled=True)  9.96 us

profile of v7, /device:TPU:1, one launch (start us, length us, event | category | flops | bytes accessed | tf_op | source)
XLA Modules:
  0.0 65.9 jit_solution(1433337751668611155)
XLA Ops:
  0.0 0.8 %spread.1 = bf16[512,128]{1,0:T(8,128)(2,1)S(1)} custom-call(s32[6]{0:T(128)} %pages_in.1, bf16[1,4096]{1,0:T(2,128)(2,1)} %query_in.1), custom_call_target="tpu_custom_call" | custom-call | tf_op jit(solution)/shard_map/spread/pallas_call | solution.py:243
  0.8 28.5 %all_to_all.26 = bf16[256,2,128]{2,1,0:T(2,128)(2,1)S(1)} all-to-all(bf16[256,2,128]{2,1,0:T(2,128)(2,1)S(1)} %bitcast.9), channel_id=1, replica_groups=mesh['req'=32,'kv'=8] {'req','kv'}, dimensions={0} | all-to-all | bytes 262144 | tf_op jit(solution)/shard_map/all_to_all | solution.py:257
  29.3 0.0 copy-start
  29.3 0.0 copy-start.1
  29.3 0.0 copy-start.2
  29.3 0.0 copy-start.3
  29.3 0.0 copy-start.4
  29.3 0.4 select.1
  29.7 11.1 %all_to_all.27 = bf16[32,3,2,128]{3,2,1,0:T(2,128)(2,1)S(1)} all-to-all(bf16[32,3,2,128]{3,2,1,0:T(2,128)(2,1)S(1)} %bitcast.12), channel_id=1, replica_groups=mesh['req'=32,'kv'=8] {'req'}, dimensions={0} | all-to-all | bytes 98304 | tf_op jit(solution)/shard_map/all_to_all | solution.py:266
  40.9 0.0 copy-done
  40.9 0.0 copy-done.1
  40.9 0.0 copy-done.2
  40.9 0.0 copy-done.3
  40.9 0.0 copy-done.4
  40.9 1.0 %attend.1 = s16[32,17,2,128]{3,2,1,0:T(2,128)(2,1)S(1)} custom-call(s32[1,6]{1,0:T(1,128)S(1)} %bitcast.13, s32[1,6]{1,0:T(1,128)S(1)} %bitcast.15, s32[1,256]{1,0:T(1,128)S(1)} %bitcast.14, bf16[192,128]{1,0:T(8,128)(2,1)S(1)} %bitcast.10, bf16[6,128,1024]{2,1,0:T(8,128)(2,1)S(1)} %copy-done, bf16[6,128,1024]{2,1,0:T(8,128)(2,1)S(1)} %copy-done.1), custom_call_target="tpu_custom_call" | custom-call | tf_op jit(solution)/shard_map/attend/pallas_call | solution.py:267
  41.9 12.6 %all_to_all.28 = s16[32,17,2,128]{3,2,1,0:T(2,128)(2,1)S(1)} all-to-all(s16[32,17,2,128]{3,2,1,0:T(2,128)(2,1)S(1)} %attend.1), channel_id=1, replica_groups=mesh['req'=32,'kv'=8] {'req'}, dimensions={0} | all-to-all | bytes 557056 | tf_op jit(solution)/shard_map/all_to_all | solution.py:280
  54.6 0.5 merge.1
  55.1 10.0 %all_to_all.29.recv = s16[8,40,128]{2,1,0:T(8,128)(2,1)S(1)} all-to-all(s16[8,40,128]{2,1,0:T(8,128)(2,1)S(1)} %merge.1), channel_id=1, replica_groups=mesh['req'=32,'kv'=8] {'kv'}, dimensions={0} | all-to-all | bytes 163840 | tf_op jit(solution)/shard_map/all_to_all | solution.py:288
  65.1 0.8 %finish.1 = bf16[1,4096]{1,0:T(2,128)(2,1)} custom-call(s16[8,40,128]{2,1,0:T(8,128)(2,1)S(1)} %all_to_all.29.recv), custom_call_target="tpu_custom_call" | custom-call | tf_op jit(solution)/shard_map/finish/pallas_call | solution.py:289
Async XLA Ops:
  29.3 11.6 %copy-start = (bf16[6,128,1024]{2,1,0:T(8,128)(2,1)S(1)}, bf16[6,128,1024]{2,1,0:T(8,128)(2,1)}, u32[]{:S(2)}) copy-start(bf16[6,128,1024]{2,1,0:T(8,128)(2,1)} %keys.1) | copy-start | bytes 4718596
  29.3 11.6 %copy-start.1 = (bf16[6,128,1024]{2,1,0:T(8,128)(2,1)S(1)}, bf16[6,128,1024]{2,1,0:T(8,128)(2,1)}, u32[]{:S(2)}) copy-start(bf16[6,128,1024]{2,1,0:T(8,128)(2,1)} %values.1) | copy-start | bytes 4718596
  29.3 11.6 %copy-start.2 = (s32[6]{0:T(128)S(1)}, s32[6]{0:T(128)}, u32[]{:S(2)}) copy-start(s32[6]{0:T(128)} %pages_in.1) | copy-start | bytes 76
  29.3 11.6 %copy-start.3 = (s32[256]{0:T(256)S(1)}, s32[256]{0:T(256)}, u32[]{:S(2)}) copy-start(s32[256]{0:T(256)} %param.11) | copy-start | bytes 3076
  29.3 11.6 %copy-start.4 = (s32[6]{0:T(128)S(1)}, s32[6]{0:T(128)}, u32[]{:S(2)}) copy-start(s32[6]{0:T(128)} %param.10) | copy-start | bytes 76
